TPU v7x, 32 devices: a whole 2x2x4 slice. The times are simulated.
32 devices in a mesh: grp: 4 (over y, x), pos: 8 (over z, core).
Axes of the slice: x: 2, y: 2, z: 4, core: 2. Of those that a mesh axis runs over, the one named last changes fastest.
Arguments:
- tiles: float32 [4, 8, 12, 256, 256], P('grp', 'pos'), may hold values from -0.109375 to 0.109375
- tile_row: int32 [4, 8, 12], P('grp', 'pos'), may hold values from 0 to 7
- tile_col: int32 [4, 8, 12], P('grp', 'pos'), may hold values from 0 to 7
- tile_count: int32 [4, 8], P('grp', 'pos'), may hold values from 1 to 12, as said below
- energies: float32 [16384], P('pos'), may hold values from 1 to 10
- basis: float32 [16, 16384], P(None, 'pos'), may hold values from -6 to 6
- prev_basis: float32 [16, 16384], P(None, 'pos'), may hold values from -6 to 6
- beta_prev: float32 [16, 16], replicated, may hold values from -3 to 3
Outputs:
- next_basis: float32 [16, 16384], P(None, 'pos')
- alpha: float32 [16, 16], replicated
- beta: float32 [16, 16], replicated
Inputs may be any that keep to these rules, and one draw needn't show every extreme that they name: `tile_count`: some segment of some diagonal uses all 12 slots in every draw.
All inputs are finite; a program needn't handle non-finite values.
Results may differ from a plain program's by a relative error of at most 0.00021.
Values sent between devices are 32-bit elements; how exact they have to be, the bound alone decides.
A program may use at most 64 MiB of HBM per device.

v0:
```python
import functools

import jax
import jax.numpy as jnp
from jax import lax
from jax.experimental import pallas as pl
from jax.experimental.pallas import tpu as pltpu
from jax.sharding import PartitionSpec as P

MESH = pl.DeviceIdType.MESH
NT = (((1,), (1,)), ((), ()))
NN = (((1,), (0,)), ((), ()))
f32 = jnp.float32
bf16 = jnp.bfloat16


def exact(left, right, dims):
    return lax.dot_general(
        left, right, dims, precision=lax.Precision.HIGHEST, preferred_element_type=f32
    )


def split(values):
    high = values.astype(bf16)
    return high, (values - high.astype(f32)).astype(bf16)


def packed(values):
    half = values.shape[0] // 2
    return jnp.concatenate([values[:half], values[half:]], axis=1)


def unpacked(values):
    half = values.shape[1] // 2
    return jnp.concatenate([values[:, :half], values[:, half:]], axis=0)


def factored(gram):
    n = gram.shape[0]
    wide = jnp.concatenate([gram, jnp.eye(n, dtype=f32)], axis=1)
    row_at = lax.broadcasted_iota(jnp.int32, (n, 1), 0)
    columns = [jnp.broadcast_to(gram[:, k : k + 1], (n, 2 * n)) for k in range(n)]
    done = jnp.zeros((n, 2 * n), f32)
    for j in range(n):
        corner = columns[j][j : j + 1]
        inverse = 1.0 / corner
        row = wide[j : j + 1]
        done = jnp.where(row_at == j, row * lax.rsqrt(corner), done)
        for k in range(j + 1, n):
            columns[k] = columns[k] - columns[j] * (columns[k][j : j + 1] * inverse)
        wide = wide - columns[j] * (row * inverse)
    return done[:, :n], done[:, n:]


def kernel(
    groups, segs,
    tiles_hbm, row_hbm, col_hbm, count_hbm, energies_hbm, basis_hbm, prev_hbm, beta_prev_hbm,
    rest_hbm, sums_ref,
    tiles, rows, cols, count, energies, own, far, prev, beta_prev,
    own_split, far_split, products, back, forth, arrived, gathered, offset, both, pair, late,
    in_sem, tile_sem, far_send, far_recv, back_send, back_recv, forth_send, forth_recv,
    gather_send, gather_recv, pair_sem, late_send, late_recv,
):
    g, p = lax.axis_index("grp"), lax.axis_index("pos")
    slots, width = tiles.shape[0], tiles.shape[-1]
    vectors, length = own.shape
    sides = length // width
    part = length // groups

    def at(group, pos):
        return (lax.rem(group + groups, groups), lax.rem(pos + segs, segs))

    def send(src, dst, send_sem, recv_sem, to):
        return pltpu.make_async_remote_copy(
            src_ref=src, dst_ref=dst, send_sem=send_sem, recv_sem=recv_sem,
            device_id=to, device_id_type=MESH,
        )

    barrier = pltpu.get_barrier_semaphore()
    greeted = 0
    for d in range(1, segs):
        pl.semaphore_signal(barrier, inc=1, device_id=at(g, p + d), device_id_type=MESH)
        greeted += 1
    for d in range(1, groups):
        pl.semaphore_signal(barrier, inc=1, device_id=at(g + d, p), device_id_type=MESH)
        source = lax.rem(g - d + groups, groups)
        pl.semaphore_signal(barrier, inc=1, device_id=at(source, p - source), device_id_type=MESH)
        pl.semaphore_signal(barrier, inc=1, device_id=at(g + d, p + g), device_id_type=MESH)
        greeted += 3

    small = [
        pltpu.make_async_copy(src, dst, in_sem.at[i])
        for i, (src, dst) in enumerate([
            (basis_hbm, own), (prev_hbm, prev), (energies_hbm, energies),
            (beta_prev_hbm, beta_prev), (row_hbm, rows), (col_hbm, cols), (count_hbm, count),
        ])
    ]
    for copy in small:
        copy.start()

    def tile_copy(k):
        return pltpu.make_async_copy(tiles_hbm.at[k], tiles.at[k], tile_sem.at[k])

    for k in range(slots):
        tile_copy(k).start()

    def stack(ref, out):
        for t in range(sides):
            high, low = split(ref[:, t * width : (t + 1) * width])
            out[t] = jnp.concatenate([high, low], axis=0)

    def multiply(picked, k, dims):
        high, low = split(tiles[k])
        both_parts = lax.dot_general(picked, high, dims, preferred_element_type=f32)
        both_parts += lax.dot_general(picked, low, dims, preferred_element_type=f32)
        return both_parts[:vectors] + both_parts[vectors:]

    def scatter(index, out):
        for t in range(sides):
            value = jnp.zeros((vectors, width), f32)
            for k in range(slots):
                live = jnp.logical_and(index[0, k] == t, k < count[0, 0])
                value = value + products[k] * jnp.where(live, 1.0, 0.0).astype(f32)
            step = min(width, part)
            for c in range(0, width, step):
                lane = t * width + c
                out[lane // part, :, lane % part : lane % part + step] = value[:, c : c + step]

    pl.semaphore_wait(barrier, greeted)

    lanes = pl.ds(pl.multiple_of(g * part, part), part)
    far_copies = []
    for d in range(groups):
        other = lax.rem(g + d, groups)
        far_copies.append(
            send(
                basis_hbm.at[:, lanes], far.at[:, lanes], far_send.at[d], far_recv.at[d],
                at(other, p - other),
            )
        )
        pl.when(other != 0)(far_copies[d].start)

    for copy in small:
        copy.wait()

    @pl.when(g == 0)
    def _():
        far[...] = own[...]

    stack(own, own_split)
    def backward(k, carry):
        tile_copy(k).wait()
        products[k] = multiply(own_split[rows[0, k]], k, NN)
        return carry

    lax.fori_loop(0, slots, backward, 0)
    scatter(cols, back)

    back_copies = []
    for d in range(groups):
        h = lax.rem(g + d, groups)
        back_copies.append(
            send(back.at[h], arrived.at[d], back_send.at[d], back_recv.at[d], at(h, p + g))
        )
    for copy in back_copies[1:]:
        copy.start()

    @pl.when(g != 0)
    def _():
        back_copies[0].start()

    @pl.when(g == 0)
    def _():
        arrived[0] = back[g]

    both[0:vectors] = own[...]
    both[vectors:] = prev[...]
    pair_slot, chip = lax.rem(p, 2), p // 2
    pair[pair_slot, :, : 4 * vectors] = packed(exact(own[...], both[...], NT))
    offset[...] = energies[...] * own[...] - exact(beta_prev[...], prev[...], NN)

    @pl.when(g != 0)
    def _():
        for copy in far_copies:
            copy.wait_recv()

    stack(far, far_split)

    def forward(k, carry):
        products[k] = multiply(far_split[cols[0, k]], k, NT)
        return carry

    lax.fori_loop(0, slots, forward, 0)
    scatter(rows, forth)

    forth_copies = []
    for d in range(1, groups):
        h = lax.rem(g + d, groups)
        forth_copies.append(
            send(forth.at[h], arrived.at[groups + d - 1], forth_send.at[d], forth_recv.at[d], at(h, p))
        )
    for copy in forth_copies:
        copy.start()
    for copy in forth_copies + back_copies[1:]:
        copy.wait_recv()

    pl.when(g != 0)(back_copies[0].wait_recv)

    mine = forth[g]
    for d in range(2 * groups - 1):
        mine = mine + arrived[d]
    gathered[g] = mine

    gather_copies = [
        send(gathered.at[g], gathered.at[g], gather_send.at[d], gather_recv.at[d], at(g + d, p))
        for d in range(1, groups)
    ]
    for copy in gather_copies:
        copy.start()
    for copy in gather_copies:
        copy.wait_recv()

    for h in range(groups):
        lanes = slice(h * part, (h + 1) * part)
        both[vectors:, lanes] = gathered[h] + offset[:, lanes]
    pair[pair_slot, :, 4 * vectors :] = packed(exact(both[vectors:], both[...], NT))

    pair_copy = send(
        pair.at[pair_slot], pair.at[pair_slot], pair_sem.at[0], pair_sem.at[1],
        at(g, p + 1 - 2 * pair_slot),
    )
    pair_copy.start()
    rest_copy = pltpu.make_async_copy(both.at[vectors:], rest_hbm, in_sem.at[0])
    rest_copy.start()
    pair_copy.wait_recv()
    late[chip] = pair[0] + pair[1]
    late_copies = [
        send(late.at[chip], late.at[chip], late_send.at[d], late_recv.at[d], at(g, p + 2 * d))
        for d in range(1, segs // 2)
    ]
    for copy in late_copies:
        copy.start()
    for copy in forth_copies + back_copies[1:] + gather_copies + [pair_copy]:
        copy.wait_send()
    pl.when(g != 0)(back_copies[0].wait_send)
    for d in range(groups):
        pl.when(lax.rem(g + d, groups) != 0)(far_copies[d].wait_send)
    for copy in late_copies:
        copy.wait()
    after = late[0]
    for s in range(1, segs // 2):
        after = after + late[s]
    sums_ref[...] = after
    rest_copy.wait()


def finish(
    total, rest_hbm, basis_hbm, sums_ref, beta_prev_ref, next_ref, alpha_ref, beta_ref, rest, basis, sem
):
    copies = [
        pltpu.make_async_copy(rest_hbm, rest, sem.at[0]),
        pltpu.make_async_copy(basis_hbm, basis, sem.at[1]),
    ]
    for copy in copies:
        copy.start()
    vectors = beta_prev_ref.shape[0]
    before = unpacked(sums_ref[:, : 4 * vectors])
    after = unpacked(sums_ref[:, 4 * vectors :])
    basis_basis, basis_prev = before[:, :vectors], before[:, vectors:]
    rest_basis, rest_rest = after[:, :vectors], after[:, vectors:]
    alpha_t = (rest_basis + exact(beta_prev_ref[...], basis_prev, NT)) / total
    alpha_ref[...] = alpha_t.T
    gram = (
        rest_rest
        + exact(exact(alpha_t, basis_basis, NN) - rest_basis, alpha_t, NT)
        - exact(alpha_t, rest_basis, NT)
    ) / total
    upper, inverse = factored(gram)
    beta_ref[...] = upper.T
    for copy in copies:
        copy.wait()
    residual = rest[...] - exact(alpha_t, basis[...], NN)
    next_ref[...] = exact(inverse, residual, NN)


def shards(groups, segs, tiles, tile_row, tile_col, tile_count, energies, basis, prev_basis, beta_prev):
    slots, width = tiles.shape[2], tiles.shape[-1]
    vectors, length = basis.shape
    sides, part = length // width, length // groups
    dma = pltpu.SemaphoreType.DMA
    block = (vectors, length)
    vmem = pl.BlockSpec(memory_space=pltpu.VMEM)
    rest, sums = pl.pallas_call(
        functools.partial(kernel, groups, segs),
        out_shape=(
            jax.ShapeDtypeStruct(block, f32),
            jax.ShapeDtypeStruct((vectors // 2, 8 * vectors), f32),
        ),
        in_specs=[pl.BlockSpec(memory_space=pltpu.HBM)] * 8,
        out_specs=(pl.BlockSpec(memory_space=pltpu.HBM), vmem),
        scratch_shapes=[
            pltpu.VMEM((slots, width, width), f32),
            pltpu.SMEM((1, slots), jnp.int32),
            pltpu.SMEM((1, slots), jnp.int32),
            pltpu.SMEM((1, 1), jnp.int32),
            pltpu.VMEM((1, length), f32),
            pltpu.VMEM(block, f32),
            pltpu.VMEM(block, f32),
            pltpu.VMEM(block, f32),
            pltpu.VMEM((vectors, vectors), f32),
            pltpu.VMEM((sides, 2 * vectors, width), bf16),
            pltpu.VMEM((sides, 2 * vectors, width), bf16),
            pltpu.VMEM((slots, vectors, width), f32),
            pltpu.VMEM((groups, vectors, part), f32),
            pltpu.VMEM((groups, vectors, part), f32),
            pltpu.VMEM((2 * groups - 1, vectors, part), f32),
            pltpu.VMEM((groups, vectors, part), f32),
            pltpu.VMEM(block, f32),
            pltpu.VMEM((2 * vectors, length), f32),
            pltpu.VMEM((2, vectors // 2, 8 * vectors), f32),
            pltpu.VMEM((segs // 2, vectors // 2, 8 * vectors), f32),
            dma((7,)), dma((slots,)), dma((groups,)), dma((groups,)),
            dma((groups,)), dma((groups,)), dma((groups,)), dma((groups,)),
            dma((groups,)), dma((groups,)),
            dma((2,)), dma((segs // 2,)), dma((segs // 2,)),
        ],
        compiler_params=pltpu.CompilerParams(collective_id=0, has_side_effects=True),
    )(
        tiles.reshape(slots, width, width),
        tile_row.reshape(1, slots),
        tile_col.reshape(1, slots),
        tile_count.reshape(1, 1),
        energies.reshape(1, length),
        basis,
        prev_basis,
        beta_prev,
    )
    return pl.pallas_call(
        functools.partial(finish, float(length * segs)),
        out_shape=(
            jax.ShapeDtypeStruct(block, f32),
            jax.ShapeDtypeStruct((vectors, vectors), f32),
            jax.ShapeDtypeStruct((vectors, vectors), f32),
        ),
        in_specs=[pl.BlockSpec(memory_space=pltpu.HBM)] * 2 + [vmem] * 2,
        out_specs=(vmem, vmem, vmem),
        scratch_shapes=[pltpu.VMEM(block, f32), pltpu.VMEM(block, f32), dma((2,))],
    )(rest, basis, sums, beta_prev)


def solution(mesh):
    groups, segs = mesh.shape["grp"], mesh.shape["pos"]
    in_specs = (
        P("grp", "pos", None, None, None),
        P("grp", "pos", None),
        P("grp", "pos", None),
        P("grp", "pos"),
        P("pos"),
        P(None, "pos"),
        P(None, "pos"),
        P(),
    )
    out_specs = (P(None, "pos"), P(), P())
    return jax.shard_map(
        functools.partial(shards, groups, segs),
        mesh=mesh, in_specs=in_specs, out_specs=out_specs, check_vma=False,
    )
```

profile of v0, /device:TPU:0, one launch (start us, length us, event | category | flops | bytes accessed | tf_op | source)
XLA Modules:
  0.0 31.2 jit_solution(2514066233809467497)
XLA Ops:
  1.3 27.0 %shard_map.103 = (f32[16,2048]{1,0:T(8,128)}, f32[8,128]{1,0:T(8,128)}) custom-call(f32[12,256,256]{2,1,0:T(8,128)} %bitcast.4, s32[1,12]{1,0:T(1,128)} %bitcast.6, s32[1,12]{1,0:T(1,128)} %bitcast.7, s32[1,1]{1,0:T(1,128)S(6)} %copy.11.count_hbm, f32[1,2048]{1,0:T(1,128)} %bitcast.5, f32[16,2048]{1,0:T(8,128)} %basis_hbm.3, f32[16,2048]{1,0:T(8,128)} %prev_hbm.1, ...), custom_call_target="tpu_custom_call" | custom-call | tf_op jit(solution)/shard_map/pallas_call | solution.py:293
  28.3 2.9 %shard_map.104 = (f32[16,2048]{1,0:T(8,128)}, f32[16,16]{1,0:T(8,128)}, f32[16,16]{1,0:T(8,128)}) custom-call(f32[16,2048]{1,0:T(8,128)} %get-tuple-element.5.rest_hbm, f32[16,2048]{1,0:T(8,128)} %basis_hbm.3, f32[8,128]{1,0:T(8,128)} %get-tuple-element.6.sums_ref, f32[16,16]{1,0:T(8,128)} %beta_prev_ref.1), custom_call_target="tpu_custom_call" | custom-call | tf_op jit(solution)/shard_map/pallas_call | solution.py:338
where the time goes:
time: 31.5 us; the launch traced here: 31.2 us
  Pallas kernels  30 us (95%)
  between operations  1.29 us (4%)
    pallas_call x1, Pallas kernels, shards(): pl.pallas_call(functools.partial(kernel, groups, segs), out_shape=(jax.Sh...  27 us
    pallas_call x1, Pallas kernels, shards(): pl.pallas_call(functools.partial(finish, float(length * segs)), out_shape...  2.95 us

commit v1 on v0

v1 whole, which is shorter than its diff:
```python
import functools

import jax
import jax.numpy as jnp
from jax import lax
from jax.experimental import pallas as pl
from jax.experimental.pallas import tpu as pltpu
from jax.sharding import PartitionSpec as P

MESH = pl.DeviceIdType.MESH
NT = (((1,), (1,)), ((), ()))
NN = (((1,), (0,)), ((), ()))
f32 = jnp.float32
bf16 = jnp.bfloat16
CORES = 2
TERMS = ((0, 0), (0, 1), (1, 0), (0, 2), (2, 0), (1, 1))


def exact(left, right, dims):
    return lax.dot_general(
        left, right, dims, precision=lax.Precision.HIGHEST, preferred_element_type=f32
    )


def split(values):
    high = values.astype(bf16)
    return high, (values - high.astype(f32)).astype(bf16)


def split3(values):
    high = values.astype(bf16)
    rest = values - high.astype(f32)
    middle = rest.astype(bf16)
    return high, middle, (rest - middle.astype(f32)).astype(bf16)


def packed(values):
    half = values.shape[0] // 2
    return jnp.concatenate([values[:half], values[half:]], axis=1)


def unpacked(values):
    half = values.shape[1] // 2
    return jnp.concatenate([values[:, :half], values[:, half:]], axis=0)


def sources(group, length):
    half, quarter = length // 2, length // 4
    low, high = group & (group - 1), group - (1 << (group.bit_length() - 1))
    if low == high:
        return [(group, 0, half), (low, half, half)]
    return [(group, 0, half), (low, half, quarter), (high, half + quarter, quarter)]


def factored(gram, extra):
    n = gram.shape[0]
    wide = jnp.concatenate([extra, gram], axis=1)
    width = wide.shape[1]
    row_at = lax.broadcasted_iota(jnp.int32, (n, 1), 0)
    columns = [jnp.broadcast_to(gram[:, k : k + 1], (n, width)) for k in range(n)]
    done = jnp.zeros((n, width), f32)
    for j in range(n):
        corner = columns[j][j : j + 1]
        inverse = 1.0 / corner
        row = wide[j : j + 1]
        done = jnp.where(row_at == j, row * lax.rsqrt(corner), done)
        for k in range(j + 1, n):
            columns[k] = columns[k] - columns[j] * (columns[k][j : j + 1] * inverse)
        wide = wide - columns[j] * (row * inverse)
    return done[:, : width - n], done[:, width - n :]


def kernel(
    groups, segs,
    tiles_hbm, row_hbm, col_hbm, count_hbm, energies_hbm, basis_hbm, prev_hbm, beta_prev_hbm,
    stack_ref, sums_ref,
    tiles, highs, lows, rows, cols, count, energies, own, far, prev, beta_prev,
    own_split, far_split, products, back, forth, arrived, rest, near, late,
    in_sem, tile_sem, far_send, far_recv, back_send, back_recv, forth_send, forth_recv,
    gather_send, gather_recv, near_send, near_recv, late_send, late_recv,
):
    g, p = lax.axis_index("grp"), lax.axis_index("pos")
    slots, width = tiles.shape[0], tiles.shape[-1]
    vectors, length = own.shape
    sides = length // width
    part = length // groups
    chips = segs // CORES
    core, chip = lax.rem(p, CORES), p // CORES
    step = next(n for n in (4, 3, 2, 1) if slots % n == 0)

    def at(group, pos):
        return (group, lax.rem(pos + segs, segs))

    def partner(d):
        other, bit = g, 1
        while bit < groups:
            if d & bit:
                other = other + bit - 2 * bit * lax.rem(g // bit, 2)
            bit *= 2
        return other

    def send(src, dst, send_sem, recv_sem, to):
        return pltpu.make_async_remote_copy(
            src_ref=src, dst_ref=dst, send_sem=send_sem, recv_sem=recv_sem,
            device_id=to, device_id_type=MESH,
        )

    mates = [(d, c) for d in reversed(range(groups)) for c in range(CORES) if d or c]

    def mate(d, c):
        return (partner(d), p + c * (1 - 2 * core))

    barrier = pltpu.get_barrier_semaphore()

    def greet(to):
        pl.semaphore_signal(barrier, inc=1, device_id=to, device_id_type=MESH)

    greeted = [0] * groups
    for mine in range(1, groups):
        for source, _, _ in sources(mine, length):
            greeted[source] += 1

        @pl.when(g == mine)
        def _():
            for source, _, _ in sources(mine, length):
                greet(at(source, p + mine))

    for d in range(1, chips):
        greet(at(g, p + CORES * d))
    for d, c in mates:
        greet(mate(d, c))
    for d in range(1, groups):
        greet(at(partner(d), p - partner(d) + segs))

    @pl.when(g != 0)
    def _():
        greet(at(g, p - g + segs))

    small = [
        pltpu.make_async_copy(src, dst, in_sem.at[i])
        for i, (src, dst) in enumerate([
            (basis_hbm, own), (prev_hbm, prev), (energies_hbm, energies),
            (beta_prev_hbm, beta_prev), (row_hbm, rows), (col_hbm, cols), (count_hbm, count),
        ])
    ]
    for copy in small:
        copy.start()

    def tile_copy(k):
        return pltpu.make_async_copy(tiles_hbm.at[k], tiles.at[k], tile_sem.at[k])

    for k in range(slots):
        tile_copy(k).start()

    def stack(ref, out):
        for t in range(sides):
            high, low = split(ref[:, t * width : (t + 1) * width])
            out[t] = jnp.concatenate([high, low], axis=0)

    def multiply(picked, high, low, dims):
        both_parts = lax.dot_general(picked, high, dims, preferred_element_type=f32)
        both_parts += lax.dot_general(picked, low, dims, preferred_element_type=f32)
        return both_parts[:vectors] + both_parts[vectors:]

    def scatter(index, out):
        for t in range(sides):
            value = jnp.zeros((vectors, width), f32)
            for k in range(slots):
                live = jnp.logical_and(index[0, k] == t, k < count[0, 0])
                value = value + products[k] * jnp.where(live, 1.0, 0.0).astype(f32)
            cut = min(width, part)
            for c in range(0, width, cut):
                lane = t * width + c
                out[lane // part, :, lane % part : lane % part + cut] = value[:, c : c + cut]

    with jax.named_scope("ph_barrier"):
        for mine in range(groups):
            expected = greeted[mine] + (chips - 1) + len(mates) + (groups - 1) + (1 if mine else 0)

            @pl.when(g == mine)
            def _():
                pl.semaphore_wait(barrier, expected)

    def far_copy(to_group, i):
        _, first, lanes = sources(to_group, length)[i]
        lanes = slice(first, first + lanes)
        return send(
            basis_hbm.at[:, lanes], far.at[:, lanes], far_send.at[to_group], far_recv.at[i],
            at(to_group, p - to_group + segs),
        )

    far_copies = [
        (source, to_group, i)
        for to_group in reversed(range(1, groups))
        for i, (source, _, _) in enumerate(sources(to_group, length))
    ]
    for source, to_group, i in far_copies:
        pl.when(g == source)(far_copy(to_group, i).start)

    with jax.named_scope("ph_small"):
        for copy in small:
            copy.wait()

    @pl.when(g == 0)
    def _():
        far[...] = own[...]

    stack(own, own_split)

    def backward(i, carry):
        for j in range(step):
            tile_copy(i * step + j).wait()
        for j in range(step):
            k = i * step + j
            high, low = split(tiles[k])
            highs[k], lows[k] = high, low
            products[k] = multiply(own_split[rows[0, k]], high, low, NN)
        return carry

    with jax.named_scope("ph_bwd"):
        lax.fori_loop(0, slots // step, backward, 0)
    with jax.named_scope("ph_scat1"):
        scatter(cols, back)

    back_copies = [
        send(back.at[partner(d)], arrived.at[d], back_send.at[d], back_recv.at[d], at(partner(d), p + g))
        for d in range(groups)
    ]
    for copy in reversed(back_copies[1:]):
        copy.start()

    @pl.when(g != 0)
    def _():
        back_copies[0].start()

    @pl.when(g == 0)
    def _():
        arrived[0] = back[g]

    with jax.named_scope("ph_pre"):
        lanes = pl.ds(pl.multiple_of(g * part, part), part)
        basis_part, prev_part = own[:, lanes], prev[:, lanes]
        own_own = exact(basis_part, basis_part, NT)
        shift = exact(beta_prev[...], exact(prev_part, basis_part, NT), NN)
        offset = energies[:, lanes] * basis_part - exact(beta_prev[...], prev_part, NN)

    with jax.named_scope("ph_farwait"):
        for mine in range(1, groups):
            @pl.when(g == mine)
            def _():
                for i in range(len(sources(mine, length))):
                    far_copy(mine, i).wait_recv()

    stack(far, far_split)

    def forward(i, carry):
        for j in range(step):
            k = i * step + j
            products[k] = multiply(far_split[cols[0, k]], highs[k], lows[k], NT)
        return carry

    with jax.named_scope("ph_fwd"):
        lax.fori_loop(0, slots // step, forward, 0)
    with jax.named_scope("ph_scat2"):
        scatter(rows, forth)

    forth_copies = [
        send(
            forth.at[partner(d)], arrived.at[groups + d - 1], forth_send.at[d], forth_recv.at[d],
            at(partner(d), p),
        )
        for d in range(1, groups)
    ]
    for copy in reversed(forth_copies):
        copy.start()
    with jax.named_scope("ph_kown"):
        pieces = split3(own[...])
        for i, (_, piece) in enumerate(TERMS):
            stack_ref[(2 * i + 1) * vectors : (2 * i + 2) * vectors, :] = pieces[piece]
    with jax.named_scope("ph_rswait"):
        for copy in forth_copies + back_copies[1:]:
            copy.wait_recv()
        pl.when(g != 0)(back_copies[0].wait_recv)

    with jax.named_scope("ph_gram"):
        mine = forth[g] + offset
        for d in range(2 * groups - 1):
            mine = mine + arrived[d]
        rest[:, lanes] = mine
        rest_own, rest_rest = exact(mine, basis_part, NT), exact(mine, mine, NT)
        slot = g * CORES + core
        near[slot] = packed(
            jnp.concatenate([own_own, rest_own + shift, rest_own, rest_rest], axis=1)
        )
    near_copies = [
        send(near.at[slot], near.at[slot], near_send.at[i], near_recv.at[i], mate(d, c))
        for i, (d, c) in enumerate(mates)
    ]
    for copy in near_copies:
        copy.start()
    gather_copies = [
        send(rest.at[:, lanes], rest.at[:, lanes], gather_send.at[d], gather_recv.at[d], at(partner(d), p))
        for d in range(1, groups)
    ]
    for copy in reversed(gather_copies):
        copy.start()
    with jax.named_scope("ph_nearwait"):
        for copy in near_copies:
            copy.wait_recv()
    total = near[0]
    for i in range(1, groups * CORES):
        total = total + near[i]
    late[chip] = total
    late_copies = [
        send(late.at[chip], late.at[chip], late_send.at[d], late_recv.at[d], at(g, p + CORES * d))
        for d in range(1, chips)
    ]
    for copy in reversed(late_copies):
        copy.start()
    with jax.named_scope("ph_gatherwait"):
        for copy in gather_copies:
            copy.wait_recv()
    with jax.named_scope("ph_krest"):
        pieces = split3(rest[...])
        for i, (_, piece) in enumerate(TERMS):
            stack_ref[2 * i * vectors : (2 * i + 1) * vectors, :] = pieces[piece]

    with jax.named_scope("ph_sendwait"):
        for copy in forth_copies + back_copies[1:] + gather_copies + near_copies:
            copy.wait_send()
        pl.when(g != 0)(back_copies[0].wait_send)
        for source, to_group, i in far_copies:
            pl.when(g == source)(far_copy(to_group, i).wait_send)
    with jax.named_scope("ph_latewait"):
        for copy in late_copies:
            copy.wait()
    total = late[0]
    for i in range(1, chips):
        total = total + late[i]
    sums_ref[...] = total


def finish(total, sums_ref, stack_ref, next_ref, alpha_ref, beta_ref):
    vectors = next_ref.shape[0]
    sums = unpacked(sums_ref[...])
    own_own, applied_own, rest_own, rest_rest = (
        sums[:, i * vectors : (i + 1) * vectors] for i in range(4)
    )
    alpha_t = applied_own / total
    alpha_ref[...] = alpha_t.T
    gram = (
        rest_rest
        + exact(exact(alpha_t, own_own, NN) - rest_own, alpha_t, NT)
        - exact(alpha_t, rest_own, NT)
    ) / total
    row_at = lax.broadcasted_iota(jnp.int32, (vectors, vectors), 0)
    col_at = lax.broadcasted_iota(jnp.int32, (vectors, vectors), 1)
    identity = jnp.where(row_at == col_at, 1.0, 0.0).astype(f32)
    with jax.named_scope("ph_factor"):
        weights, upper = factored(gram, jnp.concatenate([identity, -alpha_t], axis=1))
    beta_ref[...] = upper.T
    pieces = split3(weights)
    left = jnp.concatenate([pieces[piece] for piece, _ in TERMS], axis=1)
    with jax.named_scope("ph_last"):
        next_ref[...] = lax.dot_general(left, stack_ref[...], NN, preferred_element_type=f32)


def shards(groups, segs, tiles, tile_row, tile_col, tile_count, energies, basis, prev_basis, beta_prev):
    slots, width = tiles.shape[2], tiles.shape[-1]
    vectors, length = basis.shape
    sides, part, chips = length // width, length // groups, segs // CORES
    dma = pltpu.SemaphoreType.DMA
    block = (vectors, length)
    message = (vectors // 2, 8 * vectors)
    vmem = pl.BlockSpec(memory_space=pltpu.VMEM)
    stack, sums = pl.pallas_call(
        functools.partial(kernel, groups, segs),
        out_shape=(
            pltpu.VMEM((2 * len(TERMS) * vectors, length), bf16),
            pltpu.VMEM(message, f32),
        ),
        in_specs=[pl.BlockSpec(memory_space=pltpu.HBM)] * 8,
        out_specs=(vmem, vmem),
        scratch_shapes=[
            pltpu.VMEM((slots, width, width), f32),
            pltpu.VMEM((slots, width, width), bf16),
            pltpu.VMEM((slots, width, width), bf16),
            pltpu.SMEM((1, slots), jnp.int32),
            pltpu.SMEM((1, slots), jnp.int32),
            pltpu.SMEM((1, 1), jnp.int32),
            pltpu.VMEM((1, length), f32),
            pltpu.VMEM(block, f32),
            pltpu.VMEM(block, f32),
            pltpu.VMEM(block, f32),
            pltpu.VMEM((vectors, vectors), f32),
            pltpu.VMEM((sides, 2 * vectors, width), bf16),
            pltpu.VMEM((sides, 2 * vectors, width), bf16),
            pltpu.VMEM((slots, vectors, width), f32),
            pltpu.VMEM((groups, vectors, part), f32),
            pltpu.VMEM((groups, vectors, part), f32),
            pltpu.VMEM((2 * groups - 1, vectors, part), f32),
            pltpu.VMEM(block, f32),
            pltpu.VMEM((groups * CORES, *message), f32),
            pltpu.VMEM((chips, *message), f32),
            dma((7,)), dma((slots,)), dma((groups,)), dma((3,)),
            dma((groups,)), dma((groups,)), dma((groups,)), dma((groups,)),
            dma((groups,)), dma((groups,)),
            dma((groups * CORES,)), dma((groups * CORES,)), dma((chips,)), dma((chips,)),
        ],
        compiler_params=pltpu.CompilerParams(collective_id=0, has_side_effects=True),
    )(
        tiles.reshape(slots, width, width),
        tile_row.reshape(1, slots),
        tile_col.reshape(1, slots),
        tile_count.reshape(1, 1),
        energies.reshape(1, length),
        basis,
        prev_basis,
        beta_prev,
    )
    return pl.pallas_call(
        functools.partial(finish, float(length * segs)),
        out_shape=(
            jax.ShapeDtypeStruct(block, f32),
            jax.ShapeDtypeStruct((vectors, vectors), f32),
            jax.ShapeDtypeStruct((vectors, vectors), f32),
        ),
        in_specs=[vmem, vmem],
        out_specs=(vmem, vmem, vmem),
    )(
        pltpu.with_memory_space_constraint(sums, pltpu.VMEM),
        pltpu.with_memory_space_constraint(stack, pltpu.VMEM),
    )


def solution(mesh):
    groups, segs = mesh.shape["grp"], mesh.shape["pos"]
    in_specs = (
        P("grp", "pos", None, None, None),
        P("grp", "pos", None),
        P("grp", "pos", None),
        P("grp", "pos"),
        P("pos"),
        P(None, "pos"),
        P(None, "pos"),
        P(),
    )
    out_specs = (P(None, "pos"), P(), P())
    return jax.shard_map(
        functools.partial(shards, groups, segs),
        mesh=mesh, in_specs=in_specs, out_specs=out_specs, check_vma=False,
    )
```

time: 31.5 us -> 27.2 us (0.86)
  Pallas kernels: 30 us -> 25.8 us
    pallas_call x1, Pallas kernels: 27 us -> 24.1 us  [shards(): pl.pallas_call(functools.partial(kernel, groups, segs), out_shape=(pltpu....]
    pallas_call x1, Pallas kernels: 2.95 us -> 1.69 us  [shards(): pl.pallas_call(functools.partial(finish, float(length * segs)), out_shape...]
where the time goes in v1:
time: 27.2 us; the launch traced here: 27.1 us
  Pallas kernels  25.8 us (95%)
  between operations  1.29 us (5%)
    pallas_call x1, Pallas kernels, shards(): pl.pallas_call(functools.partial(kernel, groups, segs), out_shape=(pltpu....  24.1 us
    pallas_call x1, Pallas kernels, shards(): pl.pallas_call(functools.partial(finish, float(length * segs)), out_shape...  1.69 us

profile of v1, /device:TPU:0, one launch (start us, length us, event | category | flops | bytes accessed | tf_op | source)
XLA Modules:
  0.0 27.1 jit_solution(38223602322816419)
XLA Ops:
  1.3 24.1 %shard_map.103 = (bf16[192,2048]{1,0:T(8,128)(2,1)S(1)}, f32[8,128]{1,0:T(8,128)S(1)}) custom-call(f32[12,256,256]{2,1,0:T(8,128)} %bitcast.4, s32[1,12]{1,0:T(1,128)} %bitcast.6, s32[1,12]{1,0:T(1,128)} %bitcast.7, s32[1,1]{1,0:T(1,128)S(6)} %copy.11.count_hbm, f32[1,2048]{1,0:T(1,128)} %bitcast.5, f32[16,2048]{1,0:T(8,128)} %basis_hbm.1, ...), custom_call_target="tpu_custom_call" | custom-call | tf_op jit(solution)/shard_map/pallas_call | solution.py:376
  25.4 1.7 %shard_map.104 = (f32[16,2048]{1,0:T(8,128)}, f32[16,16]{1,0:T(8,128)}, f32[16,16]{1,0:T(8,128)}) custom-call(f32[8,128]{1,0:T(8,128)S(1)} %get-tuple-element.5.sums_ref, bf16[192,2048]{1,0:T(8,128)(2,1)S(1)} %get-tuple-element.6.stack_ref), custom_call_target="tpu_custom_call" | custom-call | tf_op jit(solution)/shard_map/pallas_call | solution.py:421

commit v2 on v1

v2 whole, which is shorter than its diff:
```python
import functools

import jax
import jax.numpy as jnp
from jax import lax
from jax.experimental import pallas as pl
from jax.experimental.pallas import tpu as pltpu
from jax.sharding import PartitionSpec as P

MESH = pl.DeviceIdType.MESH
NT = (((1,), (1,)), ((), ()))
NN = (((1,), (0,)), ((), ()))
f32 = jnp.float32
bf16 = jnp.bfloat16
CORES = 2
LANES = 128
TERMS = ((0, 0), (0, 1), (1, 0), (0, 2), (2, 0), (1, 1))


def exact(left, right, dims):
    return lax.dot_general(
        left, right, dims, precision=lax.Precision.HIGHEST, preferred_element_type=f32
    )


def split(values):
    high = values.astype(bf16)
    return high, (values - high.astype(f32)).astype(bf16)


def split3(values):
    high = values.astype(bf16)
    rest = values - high.astype(f32)
    middle = rest.astype(bf16)
    return high, middle, (rest - middle.astype(f32)).astype(bf16)


def packed(values):
    rows = values.shape[0] // 8
    return jnp.concatenate([values[i * rows : (i + 1) * rows] for i in range(8)], axis=1)


def unpacked(values):
    lanes = values.shape[1] // 8
    return jnp.concatenate([values[:, i * lanes : (i + 1) * lanes] for i in range(8)], axis=0)


def folded(values):
    rows = values.size // LANES
    return jnp.concatenate([values[i : i + rows] for i in range(0, values.shape[0], rows)], axis=1)


def unfolded(values, lanes):
    return jnp.concatenate([values[:, i : i + lanes] for i in range(0, LANES, lanes)], axis=0)


def sources(group, length):
    half, quarter = length // 2, length // 4
    low, high = group & (group - 1), group - (1 << (group.bit_length() - 1))
    if low == high:
        return [(group, 0, half), (low, half, half)]
    return [(group, 0, half), (low, half, quarter), (high, half + quarter, quarter)]


def factored(gram, extra):
    n = gram.shape[0]
    wide = jnp.concatenate([extra, gram], axis=1)
    width = wide.shape[1]
    row_at = lax.broadcasted_iota(jnp.int32, (n, 1), 0)
    columns = [jnp.broadcast_to(gram[:, k : k + 1], (n, width)) for k in range(n)]
    done = jnp.zeros((n, width), f32)
    for j in range(n):
        corner = columns[j][j : j + 1]
        inverse = 1.0 / corner
        row = wide[j : j + 1]
        done = jnp.where(row_at == j, row * lax.rsqrt(corner), done)
        for k in range(j + 1, n):
            columns[k] = columns[k] - columns[j] * (columns[k][j : j + 1] * inverse)
        wide = wide - columns[j] * (row * inverse)
    return done[:, : width - n], done[:, width - n :]


def flipped(value, d, count):
    out, bit = value, 1
    while bit < count:
        if not isinstance(d, int) or d & bit:
            out = out + (d // bit % 2) * (bit - 2 * bit * lax.rem(value // bit, 2))
        bit *= 2
    return out


def kernel(
    groups, segs, total,
    tiles_hbm, row_hbm, col_hbm, count_hbm, energies_hbm, basis_hbm, prev_hbm, beta_prev_hbm,
    stack_ref, alpha_ref, known_ref, sums_ref,
    tiles, highs, lows, rows, cols, count, energies, own, far, prev, beta_prev,
    own_split, far_split, products, back, relay, forth, arrived, rest, near, late, mids, lasts,
    in_sem, tile_sem, far_send, far_recv, sent, came, ready,
):
    g, p = lax.axis_index("grp"), lax.axis_index("pos")
    slots, width = tiles.shape[0], tiles.shape[-1]
    vectors, length = own.shape
    sides = length // width
    part = length // groups
    chips, devices = segs // CORES, groups * segs
    core, chip = lax.rem(p, CORES), p // CORES
    step = slots // tile_sem.shape[0]
    others = groups - 1
    CROSS, BACK, FORTH, GATHER, NEAR, LATE, MIDS, LASTS = range(8)

    def at(group, pos):
        return (group, lax.rem(pos + segs, segs))

    def partner(d):
        return flipped(g, d, groups)

    def send(src, dst, send_sem, recv_sem, to):
        return pltpu.make_async_remote_copy(
            src_ref=src, dst_ref=dst, send_sem=send_sem, recv_sem=recv_sem,
            device_id=to, device_id_type=MESH,
        )

    def post(which, src, dst, to):
        return send(src, dst, sent.at[which], came.at[which], to)

    def landed(which, ref):
        pltpu.make_async_copy(ref, ref, came.at[which]).wait()

    def gone(which, ref):
        pltpu.make_async_copy(ref, ref, sent.at[which]).wait()

    mates = [(d, c) for d in reversed(range(groups)) for c in range(CORES) if d or c]

    def mate(d, c):
        return (partner(d), flipped(p, c, CORES))

    barrier = pltpu.get_barrier_semaphore()

    def greet(to):
        pl.semaphore_signal(barrier, inc=1, device_id=to, device_id_type=MESH)

    greeted = [0] * groups
    for mine in range(1, groups):
        for source, _, _ in sources(mine, length):
            greeted[source] += 1

        @pl.when(g == mine)
        def _():
            for source, _, _ in sources(mine, length):
                greet(at(source, p + mine))

    column = sorted({CORES * d for d in range(1, chips)} | {segs - d for d in range(1, groups)})
    for d in column:
        greet(at(g, p + d))
    for d, c in mates:
        greet(mate(d, c))

    small = [
        pltpu.make_async_copy(src, dst, in_sem.at[i])
        for i, (src, dst) in enumerate([
            (basis_hbm, own), (row_hbm, rows), (col_hbm, cols), (count_hbm, count),
            (prev_hbm, prev), (energies_hbm, energies), (beta_prev_hbm, beta_prev),
        ])
    ]
    for copy in small:
        copy.start()

    def tile_copy(i):
        some = pl.ds(i * step, step)
        return pltpu.make_async_copy(tiles_hbm.at[some], tiles.at[some], tile_sem.at[i])

    for i in range(slots // step):
        tile_copy(i).start()

    def stack(ref, out):
        for t in range(sides):
            high, low = split(ref[:, t * width : (t + 1) * width])
            out[t] = jnp.concatenate([high, low], axis=0)

    def multiply(picked, high, low, dims):
        both_parts = lax.dot_general(picked, high, dims, preferred_element_type=f32)
        both_parts += lax.dot_general(picked, low, dims, preferred_element_type=f32)
        return both_parts[:vectors] + both_parts[vectors:]

    def scatter(index, out):
        for t in range(sides):
            value = jnp.zeros((vectors, width), f32)
            for k in range(slots):
                live = jnp.logical_and(index[0, k] == t, k < count[0, 0])
                value = value + products[k] * jnp.where(live, 1.0, 0.0).astype(f32)
            cut = min(width, part)
            for c in range(0, width, cut):
                lane = t * width + c
                out[lane // part, :, lane % part : lane % part + cut] = value[:, c : c + cut]

    def far_copy(to_group, i):
        _, first, lanes = sources(to_group, length)[i]
        lanes = slice(first, first + lanes)
        return send(
            basis_hbm.at[:, lanes], far.at[:, lanes], far_send.at[to_group], far_recv.at[i],
            at(to_group, p - to_group + segs),
        )

    far_copies = [
        (source, to_group, i)
        for to_group in reversed(range(1, groups))
        for i, (source, _, _) in enumerate(sources(to_group, length))
    ]

    def backward():
        with jax.named_scope("ph_small"):
            for copy in small:
                copy.wait()
        stack(own, own_split)

        def some(i, carry):
            tile_copy(i).wait()
            for j in range(step):
                k = i * step + j
                high, low = split(tiles[k])
                highs[k], lows[k] = high, low
                products[k] = multiply(own_split[rows[0, k]], high, low, NN)
            return carry

        with jax.named_scope("ph_bwd"):
            lax.fori_loop(0, slots // step, some, 0)
        scatter(cols, back)

    early = p < segs // 2
    pl.when(early)(backward)
    with jax.named_scope("ph_barrier"):
        for mine in range(groups):
            @pl.when(g == mine)
            def _():
                pl.semaphore_wait(barrier, greeted[mine] + len(column) + len(mates))
    for source, to_group, i in far_copies:
        pl.when(g == source)(far_copy(to_group, i).start)
    for d in range(1, chips):
        pl.semaphore_signal(ready, inc=1, device_id=at(g, p + CORES * d), device_id_type=MESH)
    pl.when(jnp.logical_not(early))(backward)

    for d in reversed(range(1, groups)):
        post(CROSS, back.at[partner(d)], relay.at[d], at(partner(d), p)).start()

    @pl.when(g == 0)
    def _():
        far[...] = own[...]

    with jax.named_scope("ph_pre"):
        lanes = pl.ds(pl.multiple_of(g * part, part), part)
        basis_part, prev_part = own[:, lanes], prev[:, lanes]
        weighted = energies[:, lanes] * basis_part
        both = jnp.concatenate([basis_part, weighted, prev_part], axis=0)
        inner = exact(both, basis_part, NT)
        inner = jnp.concatenate(
            [
                inner[: 2 * vectors],
                exact(beta_prev[...], inner[2 * vectors :], NN),
                jnp.zeros((vectors, vectors), f32),
            ],
            axis=0,
        )
        offset = weighted - exact(beta_prev[...], prev_part, NN)
        slot = g * CORES + core
        near[slot] = packed(inner)
    for d, c in mates:
        post(NEAR, near.at[slot], near.at[slot], mate(d, c)).start()

    def relay_on():
        pl.when(g != 0)(post(BACK, back.at[g], arrived.at[0], at(g, p + g)).start)
        with jax.named_scope("ph_cross"):
            landed(CROSS, relay.at[pl.ds(1, others)])
        for d in reversed(range(1, groups)):
            pl.when(g != d)(post(BACK, relay.at[d], arrived.at[d], at(g, p + partner(d))).start)
        for d in range(groups):
            @pl.when(g == d)
            def _():
                arrived[d] = relay[d] if d else back[0]

    last_chip = p >= segs - CORES
    pl.when(jnp.logical_not(last_chip))(relay_on)

    with jax.named_scope("ph_farwait"):
        for mine in range(1, groups):
            @pl.when(g == mine)
            def _():
                for i in range(len(sources(mine, length))):
                    far_copy(mine, i).wait_recv()

    stack(far, far_split)

    def forward(i, carry):
        for j in range(step):
            k = i * step + j
            products[k] = multiply(far_split[cols[0, k]], highs[k], lows[k], NT)
        return carry

    with jax.named_scope("ph_fwd"):
        lax.fori_loop(0, slots // step, forward, 0)
    with jax.named_scope("ph_scat2"):
        scatter(rows, forth)

    for d in reversed(range(1, groups)):
        post(FORTH, forth.at[partner(d)], arrived.at[groups + d - 1], at(partner(d), p)).start()
    pl.when(last_chip)(relay_on)

    def to_all(which, buffer, value):
        me = g * segs + p
        buffer[me] = value

        def copy(dg, dp):
            return post(which, buffer.at[me], buffer.at[me], (flipped(g, dg, groups), flipped(p, dp, segs)))

        if devices <= 64:
            apart = [(dp, dg) for dp in reversed(range(segs)) for dg in reversed(range(groups))]
            for dp, dg in apart[:-1]:
                copy(dg, dp).start()
        else:
            def one(d, carry):
                copy(d // segs, lax.rem(d, segs)).start()
                return carry

            lax.fori_loop(1, devices, one, 0)

    def summed(buffer):
        value = buffer[0]
        for i in range(1, buffer.shape[0]):
            value = value + buffer[i]
        return value

    with jax.named_scope("ph_mid"):
        mid = jnp.zeros((vectors, vectors), f32)
        for h in range(groups):
            mid = mid + exact(back[h], far[:, h * part : (h + 1) * part], NT)
        pl.semaphore_wait(ready, chips - 1)
        to_all(MIDS, mids, folded(mid + mid.T))

    with jax.named_scope("ph_near"):
        landed(NEAR, near.at[pl.ds(0, groups * CORES - 1)])
        late[chip] = summed(near)
    for d in reversed(range(1, chips)):
        post(LATE, late.at[chip], late.at[chip], at(g, p + CORES * d)).start()

    with jax.named_scope("ph_kown"):
        pieces = split3(own[...])
        for i, (_, piece) in enumerate(TERMS):
            stack_ref[(2 * i + 1) * vectors : (2 * i + 2) * vectors, :] = pieces[piece]
    with jax.named_scope("ph_rswait"):
        landed(BACK, arrived.at[pl.ds(0, others)])
        landed(FORTH, arrived.at[pl.ds(groups, others)])

    with jax.named_scope("ph_gram"):
        mine = forth[g] + offset
        for d in range(2 * groups - 1):
            mine = mine + arrived[d]
        rest[:, lanes] = mine
        to_all(LASTS, lasts, folded(exact(mine, mine, NT)))
    for d in reversed(range(1, groups)):
        post(GATHER, rest.at[:, lanes], rest.at[:, lanes], at(partner(d), p)).start()

    with jax.named_scope("ph_latewait"):
        landed(LATE, late.at[pl.ds(0, chips - 1)])
    with jax.named_scope("ph_gatherwait"):
        landed(GATHER, rest.at[:, pl.ds(0, others * part)])
    with jax.named_scope("ph_krest"):
        pieces = split3(rest[...])
        for i, (_, piece) in enumerate(TERMS):
            stack_ref[2 * i * vectors : (2 * i + 1) * vectors, :] = pieces[piece]
    with jax.named_scope("ph_sendwait"):
        gone(CROSS, back.at[pl.ds(0, others)])
        gone(BACK, relay.at[pl.ds(0, others)])
        gone(FORTH, forth.at[pl.ds(0, others)])
        gone(GATHER, rest.at[:, pl.ds(0, others * part)])
        gone(NEAR, near.at[pl.ds(0, groups * CORES - 1)])
        gone(LATE, late.at[pl.ds(0, chips - 1)])
        gone(MIDS, mids.at[pl.ds(0, devices - 1)])
        gone(LASTS, lasts.at[pl.ds(0, devices - 1)])
        for source, to_group, i in far_copies:
            pl.when(g == source)(far_copy(to_group, i).wait_send)
    with jax.named_scope("ph_midswait"):
        landed(MIDS, mids.at[pl.ds(0, devices - 1)])
    with jax.named_scope("ph_known"):
        inner = unpacked(summed(late))
        own_own, shift = inner[:vectors], inner[2 * vectors : 3 * vectors]
        applied_own = inner[vectors : 2 * vectors] + unfolded(summed(mids), vectors)
        rest_own, alpha_t = applied_own - shift, applied_own / total
        alpha_ref[...] = alpha_t
        known_ref[...] = (
            exact(exact(alpha_t, own_own, NN) - rest_own, alpha_t, NT) - exact(alpha_t, rest_own, NT)
        )
    with jax.named_scope("ph_lastswait"):
        landed(LASTS, lasts.at[pl.ds(0, devices - 1)])
    sums_ref[...] = summed(lasts)


def finish(total, sums_ref, alpha_t_ref, known_ref, stack_ref, next_ref, alpha_ref, beta_ref):
    vectors = next_ref.shape[0]
    alpha_t = alpha_t_ref[...]
    alpha_ref[...] = alpha_t.T
    gram = (unfolded(sums_ref[...], vectors) + known_ref[...]) / total
    row_at = lax.broadcasted_iota(jnp.int32, (vectors, vectors), 0)
    col_at = lax.broadcasted_iota(jnp.int32, (vectors, vectors), 1)
    identity = jnp.where(row_at == col_at, 1.0, 0.0).astype(f32)
    with jax.named_scope("ph_factor"):
        weights, upper = factored(gram, jnp.concatenate([identity, -alpha_t], axis=1))
    beta_ref[...] = upper.T
    pieces = split3(weights)
    left = jnp.concatenate([pieces[piece] for piece, _ in TERMS], axis=1)
    with jax.named_scope("ph_last"):
        next_ref[...] = lax.dot_general(left, stack_ref[...], NN, preferred_element_type=f32)


def shards(groups, segs, tiles, tile_row, tile_col, tile_count, energies, basis, prev_basis, beta_prev):
    slots, width = tiles.shape[2], tiles.shape[-1]
    vectors, length = basis.shape
    sides, part, chips = length // width, length // groups, segs // CORES
    step = next(n for n in (4, 3, 2, 1) if slots % n == 0)
    total = float(length * segs)
    dma = pltpu.SemaphoreType.DMA
    block, square = (vectors, length), (vectors, vectors)
    message, fold = (vectors // 2, 8 * vectors), (vectors * vectors // LANES, LANES)
    vmem = pl.BlockSpec(memory_space=pltpu.VMEM)
    stack, alpha_t, known, sums = pl.pallas_call(
        functools.partial(kernel, groups, segs, total),
        out_shape=(
            pltpu.VMEM((2 * len(TERMS) * vectors, length), bf16),
            pltpu.VMEM(square, f32),
            pltpu.VMEM(square, f32),
            pltpu.VMEM(fold, f32),
        ),
        in_specs=[pl.BlockSpec(memory_space=pltpu.HBM)] * 8,
        out_specs=(vmem,) * 4,
        scratch_shapes=[
            pltpu.VMEM((slots, width, width), f32),
            pltpu.VMEM((slots, width, width), bf16),
            pltpu.VMEM((slots, width, width), bf16),
            pltpu.SMEM((1, slots), jnp.int32),
            pltpu.SMEM((1, slots), jnp.int32),
            pltpu.SMEM((1, 1), jnp.int32),
            pltpu.VMEM((1, length), f32),
            pltpu.VMEM(block, f32),
            pltpu.VMEM(block, f32),
            pltpu.VMEM(block, f32),
            pltpu.VMEM(square, f32),
            pltpu.VMEM((sides, 2 * vectors, width), bf16),
            pltpu.VMEM((sides, 2 * vectors, width), bf16),
            pltpu.VMEM((slots, vectors, width), f32),
            pltpu.VMEM((groups, vectors, part), f32),
            pltpu.VMEM((groups, vectors, part), f32),
            pltpu.VMEM((groups, vectors, part), f32),
            pltpu.VMEM((2 * groups - 1, vectors, part), f32),
            pltpu.VMEM(block, f32),
            pltpu.VMEM((groups * CORES, *message), f32),
            pltpu.VMEM((chips, *message), f32),
            pltpu.VMEM((groups * segs, *fold), f32),
            pltpu.VMEM((groups * segs, *fold), f32),
            dma((7,)), dma((slots // step,)), dma((groups,)), dma((3,)), dma((8,)), dma((8,)),
            pltpu.SemaphoreType.REGULAR,
        ],
        compiler_params=pltpu.CompilerParams(collective_id=0, has_side_effects=True),
    )(
        tiles.reshape(slots, width, width),
        tile_row.reshape(1, slots),
        tile_col.reshape(1, slots),
        tile_count.reshape(1, 1),
        energies.reshape(1, length),
        basis,
        prev_basis,
        beta_prev,
    )
    held = [pltpu.with_memory_space_constraint(x, pltpu.VMEM) for x in (sums, alpha_t, known, stack)]
    return pl.pallas_call(
        functools.partial(finish, total),
        out_shape=(
            jax.ShapeDtypeStruct(block, f32),
            jax.ShapeDtypeStruct(square, f32),
            jax.ShapeDtypeStruct(square, f32),
        ),
        in_specs=[vmem] * 4,
        out_specs=(vmem, vmem, vmem),
    )(*held)


def solution(mesh):
    groups, segs = mesh.shape["grp"], mesh.shape["pos"]
    in_specs = (
        P("grp", "pos", None, None, None),
        P("grp", "pos", None),
        P("grp", "pos", None),
        P("grp", "pos"),
        P("pos"),
        P(None, "pos"),
        P(None, "pos"),
        P(),
    )
    out_specs = (P(None, "pos"), P(), P())
    return jax.shard_map(
        functools.partial(shards, groups, segs),
        mesh=mesh, in_specs=in_specs, out_specs=out_specs, check_vma=False,
    )
```

time: 27.2 us -> 25.3 us (0.930)
  Pallas kernels: 25.8 us -> 23.9 us
    pallas_call x2, Pallas kernels: 25.8 us -> 23.9 us  [the longest x1 22.6 us: shards(): pl.pallas_call(functools.partial(kernel, groups, segs, total), out_shape=...]
where the time goes in v2:
time: 25.3 us; the launch traced here: 25.1 us
  Pallas kernels  23.9 us (94%)
  between operations  1.29 us (5%)
    pallas_call x1, Pallas kernels, shards(): pl.pallas_call(functools.partial(kernel, groups, segs, total), out_shape=...  22.6 us
    pallas_call x1, Pallas kernels, shards(): pl.pallas_call(functools.partial(finish, total), out_shape=(jax.ShapeDtyp...  1.28 us

profile of v2, /device:TPU:0, one launch (start us, length us, event | category | flops | bytes accessed | tf_op | source)
XLA Modules:
  0.0 25.1 jit_solution(2273026509338559515)
XLA Ops:
  1.3 22.6 %shard_map.103 = (bf16[192,2048]{1,0:T(8,128)(2,1)S(1)}, f32[16,16]{1,0:T(8,128)S(1)}, f32[16,16]{1,0:T(8,128)S(1)}, f32[2,128]{1,0:T(2,128)S(1)}) custom-call(f32[12,256,256]{2,1,0:T(8,128)} %bitcast.4, s32[1,12]{1,0:T(1,128)} %bitcast.6, s32[1,12]{1,0:T(1,128)} %bitcast.7, s32[1,1]{1,0:T(1,128)S(6)} %copy.11.count_hbm, f32[1,2048]{1,0:T(1,128)} %bitcast.5, ...), custom_call_target="tpu_custom_call" | custom-call | tf_op jit(solution)/shard_map/pallas_call | solution.py:423
  23.9 1.3 %shard_map.104 = (f32[16,2048]{1,0:T(8,128)}, f32[16,16]{1,0:T(8,128)}, f32[16,16]{1,0:T(8,128)}) custom-call(f32[2,128]{1,0:T(2,128)S(1)} %get-tuple-element.7.sums_ref, f32[16,16]{1,0:T(8,128)S(1)} %get-tuple-element.8.alpha_t_ref, f32[16,16]{1,0:T(8,128)S(1)} %get-tuple-element.9.known_ref, bf16[192,2048]{1,0:T(8,128)(2,1)S(1)} %get-tuple-element.10.stack_ref), custom_call_target="tpu_custom_call" | custom-call | tf_op jit(solution)/shard_map/pallas_call | solution.py:472

commit v3 on v2

--- a/solution.py
+++ b/solution.py
@@ -58,7 +58,8 @@
     half, quarter = length // 2, length // 4
     low, high = group & (group - 1), group - (1 << (group.bit_length() - 1))
     if low == high:
-        return [(group, 0, half), (low, half, half)]
+        own = half + quarter if group == 1 else half
+        return [(group, 0, own), (low, own, length - own)]
     return [(group, 0, half), (low, half, quarter), (high, half + quarter, quarter)]
 
 
@@ -129,6 +130,12 @@
     def gone(which, ref):
         pltpu.make_async_copy(ref, ref, sent.at[which]).wait()
 
+    def settle_back(sems):
+        whole = jnp.logical_and(p >= segs - CORES, g != 0)
+        for count_of, yes in ((groups, whole), (others, jnp.logical_not(whole))):
+            ref = arrived.at[pl.ds(0, count_of)]
+            pl.when(yes)(pltpu.make_async_copy(ref, ref, sems.at[BACK]).wait)
+
     mates = [(d, c) for d in reversed(range(groups)) for c in range(CORES) if d or c]
 
     def mate(d, c):
@@ -148,6 +155,16 @@
         def _():
             for source, _, _ in sources(mine, length):
                 greet(at(source, p + mine))
+
+    last_chip = p >= segs - CORES
+
+    def of_last_chip(pos):
+        return lax.rem(pos + segs, segs) >= segs - CORES
+
+    for d in range(1, groups):
+        @pl.when(jnp.logical_and(g != d, of_last_chip(p - d)))
+        def _():
+            greet(at(d, p - d))
 
     column = sorted({CORES * d for d in range(1, chips)} | {segs - d for d in range(1, groups)})
     for d in column:
@@ -182,22 +199,34 @@
         both_parts += lax.dot_general(picked, low, dims, preferred_element_type=f32)
         return both_parts[:vectors] + both_parts[vectors:]
 
-    def scatter(index, out):
-        for t in range(sides):
-            value = jnp.zeros((vectors, width), f32)
-            for k in range(slots):
-                live = jnp.logical_and(index[0, k] == t, k < count[0, 0])
-                value = value + products[k] * jnp.where(live, 1.0, 0.0).astype(f32)
-            cut = min(width, part)
-            for c in range(0, width, cut):
-                lane = t * width + c
-                out[lane // part, :, lane % part : lane % part + cut] = value[:, c : c + cut]
+    def added(index, t):
+        value = jnp.zeros((vectors, width), f32)
+        for k in range(slots):
+            live = jnp.logical_and(index[0, k] == t, k < count[0, 0])
+            value = value + products[k] * jnp.where(live, 1.0, 0.0).astype(f32)
+        return value
+
+    def scatter(index, out, then=lambda d: None):
+        whole = part // width
+        for d in reversed(range(groups)):
+            for t in range(whole):
+                h = partner(d)
+                out[h, :, t * width : (t + 1) * width] = added(index, h * whole + t)
+            if whole:
+                then(d)
+        if not whole:
+            for t in range(sides):
+                value = added(index, t)
+                for c in range(0, width, part):
+                    out[(t * width + c) // part] = value[:, c : c + part]
+            for d in reversed(range(groups)):
+                then(d)
 
     def far_copy(to_group, i):
         _, first, lanes = sources(to_group, length)[i]
         lanes = slice(first, first + lanes)
         return send(
-            basis_hbm.at[:, lanes], far.at[:, lanes], far_send.at[to_group], far_recv.at[i],
+            own.at[:, lanes], far.at[:, lanes], far_send.at[to_group], far_recv.at[i],
             at(to_group, p - to_group + segs),
         )
 
@@ -209,7 +238,7 @@
 
     def backward():
         with jax.named_scope("ph_small"):
-            for copy in small:
+            for copy in small[1:4]:
                 copy.wait()
         stack(own, own_split)
 
@@ -227,26 +256,36 @@
         scatter(cols, back)
 
     early = p < segs // 2
+    small[0].wait()
     pl.when(early)(backward)
     with jax.named_scope("ph_barrier"):
         for mine in range(groups):
-            @pl.when(g == mine)
-            def _():
-                pl.semaphore_wait(barrier, greeted[mine] + len(column) + len(mates))
-    for source, to_group, i in far_copies:
-        pl.when(g == source)(far_copy(to_group, i).start)
+            expected = greeted[mine] + len(column) + len(mates)
+            for last in (True, False):
+                @pl.when(jnp.logical_and(g == mine, last_chip == last))
+                def _():
+                    pl.semaphore_wait(barrier, expected + (others if last and mine else 0))
+
+    for last in (True, False):
+        for source, to_group, i in far_copies:
+            turn = of_last_chip(p - to_group) == last
+            pl.when(jnp.logical_and(g == source, turn))(far_copy(to_group, i).start)
     for d in range(1, chips):
         pl.semaphore_signal(ready, inc=1, device_id=at(g, p + CORES * d), device_id_type=MESH)
     pl.when(jnp.logical_not(early))(backward)
 
-    for d in reversed(range(1, groups)):
-        post(CROSS, back.at[partner(d)], relay.at[d], at(partner(d), p)).start()
+    @pl.when(jnp.logical_not(last_chip))
+    def _():
+        for d in reversed(range(1, groups)):
+            post(CROSS, back.at[partner(d)], relay.at[d], at(partner(d), p)).start()
 
     @pl.when(g == 0)
     def _():
         far[...] = own[...]
 
     with jax.named_scope("ph_pre"):
+        for copy in small[4:]:
+            copy.wait()
         lanes = pl.ds(pl.multiple_of(g * part, part), part)
         basis_part, prev_part = own[:, lanes], prev[:, lanes]
         weighted = energies[:, lanes] * basis_part
@@ -266,19 +305,29 @@
     for d, c in mates:
         post(NEAR, near.at[slot], near.at[slot], mate(d, c)).start()
 
+    @pl.when(last_chip)
+    def _():
+        for d in reversed(range(groups)):
+            @pl.when(jnp.logical_or(g != 0, d != 0))
+            def _():
+                post(BACK, back.at[partner(d)], arrived.at[d], at(partner(d), p + g)).start()
+
+        @pl.when(g == 0)
+        def _():
+            arrived[0] = back[0]
+
     def relay_on():
-        pl.when(g != 0)(post(BACK, back.at[g], arrived.at[0], at(g, p + g)).start)
         with jax.named_scope("ph_cross"):
             landed(CROSS, relay.at[pl.ds(1, others)])
         for d in reversed(range(1, groups)):
             pl.when(g != d)(post(BACK, relay.at[d], arrived.at[d], at(g, p + partner(d))).start)
+        pl.when(g != 0)(post(BACK, back.at[g], arrived.at[0], at(g, p + g)).start)
         for d in range(groups):
             @pl.when(g == d)
             def _():
                 arrived[d] = relay[d] if d else back[0]
 
-    last_chip = p >= segs - CORES
-    pl.when(jnp.logical_not(last_chip))(relay_on)
+    pl.when(early)(relay_on)
 
     with jax.named_scope("ph_farwait"):
         for mine in range(1, groups):
@@ -289,20 +338,16 @@
 
     stack(far, far_split)
 
-    def forward(i, carry):
-        for j in range(step):
-            k = i * step + j
+    with jax.named_scope("ph_fwd"):
+        for k in range(slots):
             products[k] = multiply(far_split[cols[0, k]], highs[k], lows[k], NT)
-        return carry
-
-    with jax.named_scope("ph_fwd"):
-        lax.fori_loop(0, slots // step, forward, 0)
     with jax.named_scope("ph_scat2"):
-        scatter(rows, forth)
-
-    for d in reversed(range(1, groups)):
-        post(FORTH, forth.at[partner(d)], arrived.at[groups + d - 1], at(partner(d), p)).start()
-    pl.when(last_chip)(relay_on)
+        def pass_on(d):
+            if d:
+                post(FORTH, forth.at[partner(d)], arrived.at[groups + d - 1], at(partner(d), p)).start()
+
+        scatter(rows, forth, pass_on)
+    pl.when(jnp.logical_not(jnp.logical_or(early, last_chip)))(relay_on)
 
     def to_all(which, buffer, value):
         me = g * segs + p
@@ -312,8 +357,12 @@
             return post(which, buffer.at[me], buffer.at[me], (flipped(g, dg, groups), flipped(p, dp, segs)))
 
         if devices <= 64:
-            apart = [(dp, dg) for dp in reversed(range(segs)) for dg in reversed(range(groups))]
-            for dp, dg in apart[:-1]:
+            apart = [
+                (dp * CORES + c, dg)
+                for dp in reversed(range(chips)) for dg in reversed(range(groups)) for c in range(CORES)
+            ]
+            apart.remove((0, 0))
+            for dp, dg in apart:
                 copy(dg, dp).start()
         else:
             def one(d, carry):
@@ -346,7 +395,7 @@
         for i, (_, piece) in enumerate(TERMS):
             stack_ref[(2 * i + 1) * vectors : (2 * i + 2) * vectors, :] = pieces[piece]
     with jax.named_scope("ph_rswait"):
-        landed(BACK, arrived.at[pl.ds(0, others)])
+        settle_back(came)
         landed(FORTH, arrived.at[pl.ds(groups, others)])
 
     with jax.named_scope("ph_gram"):
@@ -354,9 +403,10 @@
         for d in range(2 * groups - 1):
             mine = mine + arrived[d]
         rest[:, lanes] = mine
-        to_all(LASTS, lasts, folded(exact(mine, mine, NT)))
-    for d in reversed(range(1, groups)):
-        post(GATHER, rest.at[:, lanes], rest.at[:, lanes], at(partner(d), p)).start()
+        value = folded(exact(mine, mine, NT))
+        for d in reversed(range(1, groups)):
+            post(GATHER, rest.at[:, lanes], rest.at[:, lanes], at(partner(d), p)).start()
+        to_all(LASTS, lasts, value)
 
     with jax.named_scope("ph_latewait"):
         landed(LATE, late.at[pl.ds(0, chips - 1)])
@@ -367,8 +417,8 @@
         for i, (_, piece) in enumerate(TERMS):
             stack_ref[2 * i * vectors : (2 * i + 1) * vectors, :] = pieces[piece]
     with jax.named_scope("ph_sendwait"):
-        gone(CROSS, back.at[pl.ds(0, others)])
-        gone(BACK, relay.at[pl.ds(0, others)])
+        pl.when(jnp.logical_not(last_chip))(lambda: gone(CROSS, back.at[pl.ds(0, others)]))
+        settle_back(sent)
         gone(FORTH, forth.at[pl.ds(0, others)])
         gone(GATHER, rest.at[:, pl.ds(0, others * part)])
         gone(NEAR, near.at[pl.ds(0, groups * CORES - 1)])

time: 25.3 us -> 23.2 us (0.917)
  Pallas kernels: 23.9 us -> 21.8 us
    pallas_call x1, Pallas kernels: 22.6 us -> 20.5 us  [shards(): pl.pallas_call(functools.partial(kernel, groups, segs, total), out_shape=...]
where the time goes in v3:
time: 23.2 us; the launch traced here: 23.1 us
  Pallas kernels  21.8 us (94%)
  between operations  1.29 us (6%)
    pallas_call x1, Pallas kernels, shards(): pl.pallas_call(functools.partial(kernel, groups, segs, total), out_shape=...  20.5 us
    pallas_call x1, Pallas kernels, shards(): pl.pallas_call(functools.partial(finish, total), out_shape=(jax.ShapeDtyp...  1.28 us

profile of v3, /device:TPU:0, one launch (start us, length us, event | category | flops | bytes accessed | tf_op | source)
XLA Modules:
  0.0 23.1 jit_solution(9265493099854274550)
XLA Ops:
  1.3 20.5 %shard_map.103 = (bf16[192,2048]{1,0:T(8,128)(2,1)S(1)}, f32[16,16]{1,0:T(8,128)S(1)}, f32[16,16]{1,0:T(8,128)S(1)}, f32[2,128]{1,0:T(2,128)S(1)}) custom-call(f32[12,256,256]{2,1,0:T(8,128)} %bitcast.4, s32[1,12]{1,0:T(1,128)} %bitcast.6, s32[1,12]{1,0:T(1,128)} %bitcast.7, s32[1,1]{1,0:T(1,128)S(6)} %copy.11.count_hbm, f32[1,2048]{1,0:T(1,128)} %bitcast.5, ...), custom_call_target="tpu_custom_call" | custom-call | tf_op jit(solution)/shard_map/pallas_call | solution.py:473
  21.8 1.3 %shard_map.104 = (f32[16,2048]{1,0:T(8,128)}, f32[16,16]{1,0:T(8,128)}, f32[16,16]{1,0:T(8,128)}) custom-call(f32[2,128]{1,0:T(2,128)S(1)} %get-tuple-element.7.sums_ref, f32[16,16]{1,0:T(8,128)S(1)} %get-tuple-element.8.alpha_t_ref, f32[16,16]{1,0:T(8,128)S(1)} %get-tuple-element.9.known_ref, bf16[192,2048]{1,0:T(8,128)(2,1)S(1)} %get-tuple-element.10.stack_ref), custom_call_target="tpu_custom_call" | custom-call | tf_op jit(solution)/shard_map/pallas_call | solution.py:522

commit v4 on v3

--- a/solution.py
+++ b/solution.py
@@ -63,22 +63,23 @@
     return [(group, 0, half), (low, half, quarter), (high, half + quarter, quarter)]
 
 
-def factored(gram, extra):
+def factored(gram, wide):
     n = gram.shape[0]
-    wide = jnp.concatenate([extra, gram], axis=1)
-    width = wide.shape[1]
+    wide = [*wide, gram]
     row_at = lax.broadcasted_iota(jnp.int32, (n, 1), 0)
-    columns = [jnp.broadcast_to(gram[:, k : k + 1], (n, width)) for k in range(n)]
-    done = jnp.zeros((n, width), f32)
+    columns = [jnp.broadcast_to(gram[:, k : k + 1], (n, LANES)) for k in range(n)]
+    done = [jnp.zeros(x.shape, f32) for x in wide]
     for j in range(n):
         corner = columns[j][j : j + 1]
-        inverse = 1.0 / corner
-        row = wide[j : j + 1]
-        done = jnp.where(row_at == j, row * lax.rsqrt(corner), done)
+        inverse, root = 1.0 / corner, lax.rsqrt(corner)
+        for i, x in enumerate(wide):
+            lanes = x.shape[1]
+            row = x[j : j + 1]
+            done[i] = jnp.where(row_at == j, row * root[:, :lanes], done[i])
+            wide[i] = x - columns[j][:, :lanes] * (row * inverse[:, :lanes])
         for k in range(j + 1, n):
             columns[k] = columns[k] - columns[j] * (columns[k][j : j + 1] * inverse)
-        wide = wide - columns[j] * (row * inverse)
-    return done[:, : width - n], done[:, width - n :]
+    return done[-1], done[:-1]
 
 
 def flipped(value, d, count):
@@ -90,13 +91,27 @@
     return out
 
 
+def sent_kib(groups, segs, vectors, length, mine, last):
+    others, block = groups - 1, vectors * length // groups // 256
+    lanes = sum(
+        n for to_group in range(1, groups)
+        for source, _, n in sources(to_group, length) if source == mine
+    )
+    blocks = (0 if last else others) + (groups if last and mine else others) + 2 * others
+    messages = groups * CORES - 1 + segs // CORES - 1
+    return (
+        lanes * vectors // 256 + blocks * block
+        + (messages * 4 * vectors + 2 * (groups * segs - 1) * vectors) * vectors // 256
+    )
+
+
 def kernel(
     groups, segs, total,
     tiles_hbm, row_hbm, col_hbm, count_hbm, energies_hbm, basis_hbm, prev_hbm, beta_prev_hbm,
-    stack_ref, alpha_ref, known_ref, sums_ref,
+    stack_ref, alpha_ref, known_ref, wide_ref, sums_ref,
     tiles, highs, lows, rows, cols, count, energies, own, far, prev, beta_prev,
     own_split, far_split, products, back, relay, forth, arrived, rest, near, late, mids, lasts,
-    in_sem, tile_sem, far_send, far_recv, sent, came, ready,
+    bulk, in_sem, tile_sem, sent, came, ready,
 ):
     g, p = lax.axis_index("grp"), lax.axis_index("pos")
     slots, width = tiles.shape[0], tiles.shape[-1]
@@ -107,7 +122,7 @@
     core, chip = lax.rem(p, CORES), p // CORES
     step = slots // tile_sem.shape[0]
     others = groups - 1
-    CROSS, BACK, FORTH, GATHER, NEAR, LATE, MIDS, LASTS = range(8)
+    FAR, CROSS, BACK, FORTH, GATHER, NEAR, LATE, MIDS, LASTS = range(9)
 
     def at(group, pos):
         return (group, lax.rem(pos + segs, segs))
@@ -122,19 +137,19 @@
         )
 
     def post(which, src, dst, to):
-        return send(src, dst, sent.at[which], came.at[which], to)
+        return send(src, dst, sent, came.at[which], to)
 
     def landed(which, ref):
         pltpu.make_async_copy(ref, ref, came.at[which]).wait()
 
-    def gone(which, ref):
-        pltpu.make_async_copy(ref, ref, sent.at[which]).wait()
-
-    def settle_back(sems):
+    def all_gone(mine, last):
+        ref = bulk.at[pl.ds(0, sent_kib(groups, segs, vectors, length, mine, last))]
+        pltpu.make_async_copy(ref, ref, sent).wait()
+
+    def settle_back():
         whole = jnp.logical_and(p >= segs - CORES, g != 0)
-        for count_of, yes in ((groups, whole), (others, jnp.logical_not(whole))):
-            ref = arrived.at[pl.ds(0, count_of)]
-            pl.when(yes)(pltpu.make_async_copy(ref, ref, sems.at[BACK]).wait)
+        pl.when(whole)(lambda: landed(BACK, arrived.at[pl.ds(0, groups)]))
+        pl.when(jnp.logical_not(whole))(lambda: landed(BACK, arrived.at[pl.ds(0, others)]))
 
     mates = [(d, c) for d in reversed(range(groups)) for c in range(CORES) if d or c]
 
@@ -225,10 +240,7 @@
     def far_copy(to_group, i):
         _, first, lanes = sources(to_group, length)[i]
         lanes = slice(first, first + lanes)
-        return send(
-            own.at[:, lanes], far.at[:, lanes], far_send.at[to_group], far_recv.at[i],
-            at(to_group, p - to_group + segs),
-        )
+        return post(FAR, own.at[:, lanes], far.at[:, lanes], at(to_group, p - to_group + segs))
 
     far_copies = [
         (source, to_group, i)
@@ -330,11 +342,7 @@
     pl.when(early)(relay_on)
 
     with jax.named_scope("ph_farwait"):
-        for mine in range(1, groups):
-            @pl.when(g == mine)
-            def _():
-                for i in range(len(sources(mine, length))):
-                    far_copy(mine, i).wait_recv()
+        pl.when(g != 0)(lambda: landed(FAR, far))
 
     stack(far, far_split)
 
@@ -395,7 +403,7 @@
         for i, (_, piece) in enumerate(TERMS):
             stack_ref[(2 * i + 1) * vectors : (2 * i + 2) * vectors, :] = pieces[piece]
     with jax.named_scope("ph_rswait"):
-        settle_back(came)
+        settle_back()
         landed(FORTH, arrived.at[pl.ds(groups, others)])
 
     with jax.named_scope("ph_gram"):
@@ -417,16 +425,11 @@
         for i, (_, piece) in enumerate(TERMS):
             stack_ref[2 * i * vectors : (2 * i + 1) * vectors, :] = pieces[piece]
     with jax.named_scope("ph_sendwait"):
-        pl.when(jnp.logical_not(last_chip))(lambda: gone(CROSS, back.at[pl.ds(0, others)]))
-        settle_back(sent)
-        gone(FORTH, forth.at[pl.ds(0, others)])
-        gone(GATHER, rest.at[:, pl.ds(0, others * part)])
-        gone(NEAR, near.at[pl.ds(0, groups * CORES - 1)])
-        gone(LATE, late.at[pl.ds(0, chips - 1)])
-        gone(MIDS, mids.at[pl.ds(0, devices - 1)])
-        gone(LASTS, lasts.at[pl.ds(0, devices - 1)])
-        for source, to_group, i in far_copies:
-            pl.when(g == source)(far_copy(to_group, i).wait_send)
+        for mine in range(groups):
+            for last in (True, False):
+                @pl.when(jnp.logical_and(g == mine, last_chip == last))
+                def _():
+                    all_gone(mine, last)
     with jax.named_scope("ph_midswait"):
         landed(MIDS, mids.at[pl.ds(0, devices - 1)])
     with jax.named_scope("ph_known"):
@@ -435,6 +438,10 @@
         applied_own = inner[vectors : 2 * vectors] + unfolded(summed(mids), vectors)
         rest_own, alpha_t = applied_own - shift, applied_own / total
         alpha_ref[...] = alpha_t
+        row_at = lax.broadcasted_iota(jnp.int32, (vectors, vectors), 0)
+        col_at = lax.broadcasted_iota(jnp.int32, (vectors, vectors), 1)
+        identity = jnp.where(row_at == col_at, 1.0, 0.0).astype(f32)
+        wide_ref[...] = jnp.concatenate([identity, -alpha_t] * len(TERMS), axis=1)
         known_ref[...] = (
             exact(exact(alpha_t, own_own, NN) - rest_own, alpha_t, NT) - exact(alpha_t, rest_own, NT)
         )
@@ -443,21 +450,39 @@
     sums_ref[...] = summed(lasts)
 
 
-def finish(total, sums_ref, alpha_t_ref, known_ref, stack_ref, next_ref, alpha_ref, beta_ref):
-    vectors = next_ref.shape[0]
-    alpha_t = alpha_t_ref[...]
-    alpha_ref[...] = alpha_t.T
+def finish(
+    total, sums_ref, alpha_t_ref, known_ref, wide_ref, stack_ref, next_hbm, alpha_hbm, beta_hbm,
+    ahead, alpha, beta, sem,
+):
+    vectors, length = ahead.shape
+    alpha[...] = alpha_t_ref[...].T
+    outs = [pltpu.make_async_copy(alpha, alpha_hbm, sem.at[0]), pltpu.make_async_copy(beta, beta_hbm, sem.at[1])]
+    outs[0].start()
     gram = (unfolded(sums_ref[...], vectors) + known_ref[...]) / total
-    row_at = lax.broadcasted_iota(jnp.int32, (vectors, vectors), 0)
-    col_at = lax.broadcasted_iota(jnp.int32, (vectors, vectors), 1)
-    identity = jnp.where(row_at == col_at, 1.0, 0.0).astype(f32)
+    cuts = [slice(i, min(i + LANES, wide_ref.shape[1])) for i in range(0, wide_ref.shape[1], LANES)]
     with jax.named_scope("ph_factor"):
-        weights, upper = factored(gram, jnp.concatenate([identity, -alpha_t], axis=1))
-    beta_ref[...] = upper.T
-    pieces = split3(weights)
-    left = jnp.concatenate([pieces[piece] for piece, _ in TERMS], axis=1)
+        upper, weights = factored(gram, [wide_ref[:, cut] for cut in cuts])
+    left = []
+    for cut, values in zip(cuts, weights, strict=True):
+        pieces = split3(values)
+        term = lax.broadcasted_iota(jnp.int32, values.shape, 1) // (2 * vectors) + cut.start // (2 * vectors)
+        value = pieces[0].astype(f32)
+        for i, (piece, _) in enumerate(TERMS):
+            if piece:
+                value = jnp.where(term == i, pieces[piece].astype(f32), value)
+        left.append(value.astype(bf16))
+    left = jnp.concatenate(left, axis=1)
     with jax.named_scope("ph_last"):
-        next_ref[...] = lax.dot_general(left, stack_ref[...], NN, preferred_element_type=f32)
+        half = length // 2
+        for i in range(2):
+            lanes = slice(i * half, (i + 1) * half)
+            ahead[:, lanes] = lax.dot_general(left, stack_ref[:, lanes], NN, preferred_element_type=f32)
+            outs.append(pltpu.make_async_copy(ahead.at[:, lanes], next_hbm.at[:, lanes], sem.at[2 + i]))
+            outs[-1].start()
+    beta[...] = upper.T
+    outs[1].start()
+    for copy in outs:
+        copy.wait()
 
 
 def shards(groups, segs, tiles, tile_row, tile_col, tile_count, energies, basis, prev_basis, beta_prev):
@@ -469,17 +494,22 @@
     dma = pltpu.SemaphoreType.DMA
     block, square = (vectors, length), (vectors, vectors)
     message, fold = (vectors // 2, 8 * vectors), (vectors * vectors // LANES, LANES)
+    kib = max(
+        sent_kib(groups, segs, vectors, length, mine, last)
+        for mine in range(groups) for last in (True, False)
+    )
     vmem = pl.BlockSpec(memory_space=pltpu.VMEM)
-    stack, alpha_t, known, sums = pl.pallas_call(
+    stack, alpha_t, known, wide, sums = pl.pallas_call(
         functools.partial(kernel, groups, segs, total),
         out_shape=(
             pltpu.VMEM((2 * len(TERMS) * vectors, length), bf16),
             pltpu.VMEM(square, f32),
             pltpu.VMEM(square, f32),
+            pltpu.VMEM((vectors, 2 * len(TERMS) * vectors), f32),
             pltpu.VMEM(fold, f32),
         ),
         in_specs=[pl.BlockSpec(memory_space=pltpu.HBM)] * 8,
-        out_specs=(vmem,) * 4,
+        out_specs=(vmem,) * 5,
         scratch_shapes=[
             pltpu.VMEM((slots, width, width), f32),
             pltpu.VMEM((slots, width, width), bf16),
@@ -504,7 +534,8 @@
             pltpu.VMEM((chips, *message), f32),
             pltpu.VMEM((groups * segs, *fold), f32),
             pltpu.VMEM((groups * segs, *fold), f32),
-            dma((7,)), dma((slots // step,)), dma((groups,)), dma((3,)), dma((8,)), dma((8,)),
+            pltpu.VMEM((kib, *fold), f32),
+            dma((7,)), dma((slots // step,)), dma, dma((9,)),
             pltpu.SemaphoreType.REGULAR,
         ],
         compiler_params=pltpu.CompilerParams(collective_id=0, has_side_effects=True),
@@ -518,7 +549,7 @@
         prev_basis,
         beta_prev,
     )
-    held = [pltpu.with_memory_space_constraint(x, pltpu.VMEM) for x in (sums, alpha_t, known, stack)]
+    held = [pltpu.with_memory_space_constraint(x, pltpu.VMEM) for x in (sums, alpha_t, known, wide, stack)]
     return pl.pallas_call(
         functools.partial(finish, total),
         out_shape=(
@@ -526,8 +557,9 @@
             jax.ShapeDtypeStruct(square, f32),
             jax.ShapeDtypeStruct(square, f32),
         ),
-        in_specs=[vmem] * 4,
-        out_specs=(vmem, vmem, vmem),
+        in_specs=[vmem] * 5,
+        out_specs=(pl.BlockSpec(memory_space=pltpu.HBM),) * 3,
+        scratch_shapes=[pltpu.VMEM(block, f32), pltpu.VMEM(square, f32), pltpu.VMEM(square, f32), dma((4,))],
     )(*held)
 
 

time: 23.2 us -> 23 us (level)
  no operation moved by 1% of the time
where the time goes in v4:
time: 23 us; the launch traced here: 22.9 us
  Pallas kernels  21.6 us (94%)
  between operations  1.29 us (6%)
    pallas_call x1, Pallas kernels, shards(): pl.pallas_call(functools.partial(kernel, groups, segs, total), out_shape=...  20.4 us
    pallas_call x1, Pallas kernels, shards(): pl.pallas_call(functools.partial(finish, total), out_shape=(jax.ShapeDtyp...  1.2 us

profile of v4, /device:TPU:0, one launch (start us, length us, event | category | flops | bytes accessed | tf_op | source)
XLA Modules:
  0.0 22.9 jit_solution(16867173060447567908)
XLA Ops:
  1.3 20.4 %shard_map.103 = (bf16[192,2048]{1,0:T(8,128)(2,1)S(1)}, f32[16,16]{1,0:T(8,128)S(1)}, f32[16,16]{1,0:T(8,128)S(1)}, f32[16,192]{1,0:T(8,128)S(1)}, f32[2,128]{1,0:T(2,128)S(1)}) custom-call(f32[12,256,256]{2,1,0:T(8,128)} %bitcast.4, s32[1,12]{1,0:T(1,128)} %bitcast.6, s32[1,12]{1,0:T(1,128)} %bitcast.7, s32[1,1]{1,0:T(1,128)S(6)} %copy.11.count_hbm, ...), custom_call_target="tpu_custom_call" | custom-call | tf_op jit(solution)/shard_map/pallas_call | solution.py:502
  21.7 1.2 %shard_map.104 = (f32[16,2048]{1,0:T(8,128)}, f32[16,16]{1,0:T(8,128)}, f32[16,16]{1,0:T(8,128)}) custom-call(f32[2,128]{1,0:T(2,128)S(1)} %get-tuple-element.8.sums_ref, f32[16,16]{1,0:T(8,128)S(1)} %get-tuple-element.9.alpha_t_ref, f32[16,16]{1,0:T(8,128)S(1)} %get-tuple-element.10.known_ref, f32[16,192]{1,0:T(8,128)S(1)} %get-tuple-element.11.wide_ref, ...), custom_call_target="tpu_custom_call" | custom-call | tf_op jit(solution)/shard_map/pallas_call | solution.py:553

commit v5 on v4

--- a/solution.py
+++ b/solution.py
@@ -259,7 +259,6 @@
             for j in range(step):
                 k = i * step + j
                 high, low = split(tiles[k])
-                highs[k], lows[k] = high, low
                 products[k] = multiply(own_split[rows[0, k]], high, low, NN)
             return carry
 
@@ -328,6 +327,17 @@
         def _():
             arrived[0] = back[0]
 
+    pairs = 2 if slots % 2 == 0 else 1
+
+    def turn(i, carry):
+        for j in range(pairs):
+            k = i * pairs + j
+            highs[k], lows[k] = split(tiles[k].T)
+        return carry
+
+    with jax.named_scope("ph_turn"):
+        lax.fori_loop(0, slots // pairs, turn, 0)
+
     def relay_on():
         with jax.named_scope("ph_cross"):
             landed(CROSS, relay.at[pl.ds(1, others)])
@@ -348,7 +358,7 @@
 
     with jax.named_scope("ph_fwd"):
         for k in range(slots):
-            products[k] = multiply(far_split[cols[0, k]], highs[k], lows[k], NT)
+            products[k] = multiply(far_split[cols[0, k]], highs[k], lows[k], NN)
     with jax.named_scope("ph_scat2"):
         def pass_on(d):
             if d:

time: 23 us -> 22.6 us (0.983)
  Pallas kernels: 21.6 us -> 21.2 us
    pallas_call x1, Pallas kernels: 20.4 us -> 20 us  [shards(): pl.pallas_call(functools.partial(kernel, groups, segs, total), out_shape=...]
where the time goes in v5:
time: 22.6 us; the launch traced here: 22.5 us
  Pallas kernels  21.2 us (94%)
  between operations  1.29 us (6%)
    pallas_call x1, Pallas kernels, shards(): pl.pallas_call(functools.partial(kernel, groups, segs, total), out_shape=...  20 us
    pallas_call x1, Pallas kernels, shards(): pl.pallas_call(functools.partial(finish, total), out_shape=(jax.ShapeDtyp...  1.2 us

profile of v5, /device:TPU:0, one launch (start us, length us, event | category | flops | bytes accessed | tf_op | source)
XLA Modules:
  0.0 22.5 jit_solution(8379041895609658248)
XLA Ops:
  1.3 20.0 %shard_map.103 = (bf16[192,2048]{1,0:T(8,128)(2,1)S(1)}, f32[16,16]{1,0:T(8,128)S(1)}, f32[16,16]{1,0:T(8,128)S(1)}, f32[16,192]{1,0:T(8,128)S(1)}, f32[2,128]{1,0:T(2,128)S(1)}) custom-call(f32[12,256,256]{2,1,0:T(8,128)} %bitcast.4, s32[1,12]{1,0:T(1,128)} %bitcast.6, s32[1,12]{1,0:T(1,128)} %bitcast.7, s32[1,1]{1,0:T(1,128)S(6)} %copy.11.count_hbm, ...), custom_call_target="tpu_custom_call" | custom-call | tf_op jit(solution)/shard_map/pallas_call | solution.py:512
  21.3 1.2 %shard_map.104 = (f32[16,2048]{1,0:T(8,128)}, f32[16,16]{1,0:T(8,128)}, f32[16,16]{1,0:T(8,128)}) custom-call(f32[2,128]{1,0:T(2,128)S(1)} %get-tuple-element.8.sums_ref, f32[16,16]{1,0:T(8,128)S(1)} %get-tuple-element.9.alpha_t_ref, f32[16,16]{1,0:T(8,128)S(1)} %get-tuple-element.10.known_ref, f32[16,192]{1,0:T(8,128)S(1)} %get-tuple-element.11.wide_ref, ...), custom_call_target="tpu_custom_call" | custom-call | tf_op jit(solution)/shard_map/pallas_call | solution.py:563

commit v6 on v5

--- a/solution.py
+++ b/solution.py
@@ -101,7 +101,7 @@
     messages = groups * CORES - 1 + segs // CORES - 1
     return (
         lanes * vectors // 256 + blocks * block
-        + (messages * 4 * vectors + 2 * (groups * segs - 1) * vectors) * vectors // 256
+        + (messages * 5 * vectors + (groups * segs - 1) * vectors) * vectors // 256
     )
 
 
@@ -110,7 +110,7 @@
     tiles_hbm, row_hbm, col_hbm, count_hbm, energies_hbm, basis_hbm, prev_hbm, beta_prev_hbm,
     stack_ref, alpha_ref, known_ref, wide_ref, sums_ref,
     tiles, highs, lows, rows, cols, count, energies, own, far, prev, beta_prev,
-    own_split, far_split, products, back, relay, forth, arrived, rest, near, late, mids, lasts,
+    own_split, far_split, products, back, relay, forth, arrived, rest, near, late, mids, ends, lasts,
     bulk, in_sem, tile_sem, sent, came, ready,
 ):
     g, p = lax.axis_index("grp"), lax.axis_index("pos")
@@ -122,7 +122,7 @@
     core, chip = lax.rem(p, CORES), p // CORES
     step = slots // tile_sem.shape[0]
     others = groups - 1
-    FAR, CROSS, BACK, FORTH, GATHER, NEAR, LATE, MIDS, LASTS = range(9)
+    FAR, CROSS, BACK, FORTH, GATHER, NEAR, LATE, MIDS, ENDS, LASTS = range(10)
 
     def at(group, pos):
         return (group, lax.rem(pos + segs, segs))
@@ -399,8 +399,9 @@
         mid = jnp.zeros((vectors, vectors), f32)
         for h in range(groups):
             mid = mid + exact(back[h], far[:, h * part : (h + 1) * part], NT)
-        pl.semaphore_wait(ready, chips - 1)
-        to_all(MIDS, mids, folded(mid + mid.T))
+        mids[chip] = folded(mid + mid.T)
+    for d in reversed(range(1, chips)):
+        post(MIDS, mids.at[chip], mids.at[chip], at(g, p + CORES * d)).start()
 
     with jax.named_scope("ph_near"):
         landed(NEAR, near.at[pl.ds(0, groups * CORES - 1)])
@@ -417,6 +418,7 @@
         landed(FORTH, arrived.at[pl.ds(groups, others)])
 
     with jax.named_scope("ph_gram"):
+        pl.semaphore_wait(ready, chips - 1)
         mine = forth[g] + offset
         for d in range(2 * groups - 1):
             mine = mine + arrived[d]
@@ -428,6 +430,11 @@
 
     with jax.named_scope("ph_latewait"):
         landed(LATE, late.at[pl.ds(0, chips - 1)])
+    with jax.named_scope("ph_mids1"):
+        landed(MIDS, mids.at[pl.ds(0, chips - 1)])
+        ends[slot] = summed(mids)
+    for d, c in mates:
+        post(ENDS, ends.at[slot], ends.at[slot], mate(d, c)).start()
     with jax.named_scope("ph_gatherwait"):
         landed(GATHER, rest.at[:, pl.ds(0, others * part)])
     with jax.named_scope("ph_krest"):
@@ -441,11 +448,11 @@
                 def _():
                     all_gone(mine, last)
     with jax.named_scope("ph_midswait"):
-        landed(MIDS, mids.at[pl.ds(0, devices - 1)])
+        landed(ENDS, ends.at[pl.ds(0, groups * CORES - 1)])
     with jax.named_scope("ph_known"):
         inner = unpacked(summed(late))
         own_own, shift = inner[:vectors], inner[2 * vectors : 3 * vectors]
-        applied_own = inner[vectors : 2 * vectors] + unfolded(summed(mids), vectors)
+        applied_own = inner[vectors : 2 * vectors] + unfolded(summed(ends), vectors)
         rest_own, alpha_t = applied_own - shift, applied_own / total
         alpha_ref[...] = alpha_t
         row_at = lax.broadcasted_iota(jnp.int32, (vectors, vectors), 0)
@@ -489,8 +496,9 @@
             ahead[:, lanes] = lax.dot_general(left, stack_ref[:, lanes], NN, preferred_element_type=f32)
             outs.append(pltpu.make_async_copy(ahead.at[:, lanes], next_hbm.at[:, lanes], sem.at[2 + i]))
             outs[-1].start()
-    beta[...] = upper.T
-    outs[1].start()
+            if i == 0:
+                beta[...] = upper.T
+                outs[1].start()
     for copy in outs:
         copy.wait()
 
@@ -542,10 +550,11 @@
             pltpu.VMEM(block, f32),
             pltpu.VMEM((groups * CORES, *message), f32),
             pltpu.VMEM((chips, *message), f32),
-            pltpu.VMEM((groups * segs, *fold), f32),
+            pltpu.VMEM((chips, *fold), f32),
+            pltpu.VMEM((groups * CORES, *fold), f32),
             pltpu.VMEM((groups * segs, *fold), f32),
             pltpu.VMEM((kib, *fold), f32),
-            dma((7,)), dma((slots // step,)), dma, dma((9,)),
+            dma((7,)), dma((slots // step,)), dma, dma((10,)),
             pltpu.SemaphoreType.REGULAR,
         ],
         compiler_params=pltpu.CompilerParams(collective_id=0, has_side_effects=True),

time: 22.6 us -> 22.5 us (level)
  no operation moved by 1% of the time
where the time goes in v6:
time: 22.5 us; the launch traced here: 22.4 us
  Pallas kernels  21.1 us (94%)
  between operations  1.29 us (6%)
    pallas_call x1, Pallas kernels, shards(): pl.pallas_call(functools.partial(kernel, groups, segs, total), out_shape=...  19.9 us
    pallas_call x1, Pallas kernels, shards(): pl.pallas_call(functools.partial(finish, total), out_shape=(jax.ShapeDtyp...  1.2 us

profile of v6, /device:TPU:0, one launch (start us, length us, event | category | flops | bytes accessed | tf_op | source)
XLA Modules:
  0.0 22.4 jit_solution(5956730491208745003)
XLA Ops:
  1.3 19.9 %shard_map.103 = (bf16[192,2048]{1,0:T(8,128)(2,1)S(1)}, f32[16,16]{1,0:T(8,128)S(1)}, f32[16,16]{1,0:T(8,128)S(1)}, f32[16,192]{1,0:T(8,128)S(1)}, f32[2,128]{1,0:T(2,128)S(1)}) custom-call(f32[12,256,256]{2,1,0:T(8,128)} %bitcast.4, s32[1,12]{1,0:T(1,128)} %bitcast.6, s32[1,12]{1,0:T(1,128)} %bitcast.7, s32[1,1]{1,0:T(1,128)S(6)} %copy.11.count_hbm, ...), custom_call_target="tpu_custom_call" | custom-call | tf_op jit(solution)/shard_map/pallas_call | solution.py:520
  21.2 1.2 %shard_map.104 = (f32[16,2048]{1,0:T(8,128)}, f32[16,16]{1,0:T(8,128)}, f32[16,16]{1,0:T(8,128)}) custom-call(f32[2,128]{1,0:T(2,128)S(1)} %get-tuple-element.8.sums_ref, f32[16,16]{1,0:T(8,128)S(1)} %get-tuple-element.9.alpha_t_ref, f32[16,16]{1,0:T(8,128)S(1)} %get-tuple-element.10.known_ref, f32[16,192]{1,0:T(8,128)S(1)} %get-tuple-element.11.wide_ref, ...), custom_call_target="tpu_custom_call" | custom-call | tf_op jit(solution)/shard_map/pallas_call | solution.py:572

commit v7 on v6

--- a/solution.py
+++ b/solution.py
@@ -266,21 +266,22 @@
             lax.fori_loop(0, slots // step, some, 0)
         scatter(cols, back)
 
-    early = p < segs // 2
+    early = p < CORES
     small[0].wait()
     pl.when(early)(backward)
     with jax.named_scope("ph_barrier"):
-        for mine in range(groups):
-            expected = greeted[mine] + len(column) + len(mates)
-            for last in (True, False):
-                @pl.when(jnp.logical_and(g == mine, last_chip == last))
-                def _():
-                    pl.semaphore_wait(barrier, expected + (others if last and mine else 0))
-
-    for last in (True, False):
-        for source, to_group, i in far_copies:
-            turn = of_last_chip(p - to_group) == last
-            pl.when(jnp.logical_and(g == source, turn))(far_copy(to_group, i).start)
+        for mine in reversed(range(groups)):
+            @pl.when(g == mine)
+            def _():
+                expected = greeted[mine] + len(column) + len(mates)
+                for last in (False, True):
+                    pl.when(last_chip == last)(
+                        functools.partial(pl.semaphore_wait, barrier, expected + (others if last and mine else 0))
+                    )
+                for last in (True, False):
+                    for source, to_group, i in far_copies:
+                        if source == mine:
+                            pl.when(of_last_chip(p - to_group) == last)(far_copy(to_group, i).start)
     for d in range(1, chips):
         pl.semaphore_signal(ready, inc=1, device_id=at(g, p + CORES * d), device_id_type=MESH)
     pl.when(jnp.logical_not(early))(backward)
@@ -349,7 +350,7 @@
             def _():
                 arrived[d] = relay[d] if d else back[0]
 
-    pl.when(early)(relay_on)
+    pl.when(p < segs // 2)(relay_on)
 
     with jax.named_scope("ph_farwait"):
         pl.when(g != 0)(lambda: landed(FAR, far))
@@ -365,7 +366,7 @@
                 post(FORTH, forth.at[partner(d)], arrived.at[groups + d - 1], at(partner(d), p)).start()
 
         scatter(rows, forth, pass_on)
-    pl.when(jnp.logical_not(jnp.logical_or(early, last_chip)))(relay_on)
+    pl.when(jnp.logical_not(jnp.logical_or(p < segs // 2, last_chip)))(relay_on)
 
     def to_all(which, buffer, value):
         me = g * segs + p

time: 22.5 us -> 22.5 us (level)
  no operation moved by 1% of the time
where the time goes in v7:
time: 22.5 us; the launch traced here: 22.4 us
  Pallas kernels  21.1 us (94%)
  between operations  1.29 us (6%)
    pallas_call x1, Pallas kernels, shards(): pl.pallas_call(functools.partial(kernel, groups, segs, total), out_shape=...  19.9 us
    pallas_call x1, Pallas kernels, shards(): pl.pallas_call(functools.partial(finish, total), out_shape=(jax.ShapeDtyp...  1.2 us

profile of v7, /device:TPU:0, one launch (start us, length us, event | category | flops | bytes accessed | tf_op | source)
XLA Modules:
  0.0 22.4 jit_solution(203795307584078986)
XLA Ops:
  1.3 19.9 %shard_map.103 = (bf16[192,2048]{1,0:T(8,128)(2,1)S(1)}, f32[16,16]{1,0:T(8,128)S(1)}, f32[16,16]{1,0:T(8,128)S(1)}, f32[16,192]{1,0:T(8,128)S(1)}, f32[2,128]{1,0:T(2,128)S(1)}) custom-call(f32[12,256,256]{2,1,0:T(8,128)} %bitcast.4, s32[1,12]{1,0:T(1,128)} %bitcast.6, s32[1,12]{1,0:T(1,128)} %bitcast.7, s32[1,1]{1,0:T(1,128)S(6)} %copy.11.count_hbm, ...), custom_call_target="tpu_custom_call" | custom-call | tf_op jit(solution)/shard_map/pallas_call | solution.py:521
  21.2 1.2 %shard_map.104 = (f32[16,2048]{1,0:T(8,128)}, f32[16,16]{1,0:T(8,128)}, f32[16,16]{1,0:T(8,128)}) custom-call(f32[2,128]{1,0:T(2,128)S(1)} %get-tuple-element.8.sums_ref, f32[16,16]{1,0:T(8,128)S(1)} %get-tuple-element.9.alpha_t_ref, f32[16,16]{1,0:T(8,128)S(1)} %get-tuple-element.10.known_ref, f32[16,192]{1,0:T(8,128)S(1)} %get-tuple-element.11.wide_ref, ...), custom_call_target="tpu_custom_call" | custom-call | tf_op jit(solution)/shard_map/pallas_call | solution.py:573

commit v8 on v7

--- a/solution.py
+++ b/solution.py
@@ -423,11 +423,11 @@
         mine = forth[g] + offset
         for d in range(2 * groups - 1):
             mine = mine + arrived[d]
+        value = folded(exact(mine, mine, NT))
+        to_all(LASTS, lasts, value)
         rest[:, lanes] = mine
-        value = folded(exact(mine, mine, NT))
         for d in reversed(range(1, groups)):
             post(GATHER, rest.at[:, lanes], rest.at[:, lanes], at(partner(d), p)).start()
-        to_all(LASTS, lasts, value)
 
     with jax.named_scope("ph_latewait"):
         landed(LATE, late.at[pl.ds(0, chips - 1)])

time: 22.5 us -> 22.5 us (level)
  no operation moved by 1% of the time
where the time goes in v8:
time: 22.5 us; the launch traced here: 22.4 us
  Pallas kernels  21.1 us (94%)
  between operations  1.29 us (6%)
    pallas_call x1, Pallas kernels, shards(): pl.pallas_call(functools.partial(kernel, groups, segs, total), out_shape=...  19.9 us
    pallas_call x1, Pallas kernels, shards(): pl.pallas_call(functools.partial(finish, total), out_shape=(jax.ShapeDtyp...  1.2 us

profile of v8, /device:TPU:0, one launch (start us, length us, event | category | flops | bytes accessed | tf_op | source)
XLA Modules:
  0.0 22.4 jit_solution(17601404144566096234)
XLA Ops:
  1.3 19.9 %shard_map.103 = (bf16[192,2048]{1,0:T(8,128)(2,1)S(1)}, f32[16,16]{1,0:T(8,128)S(1)}, f32[16,16]{1,0:T(8,128)S(1)}, f32[16,192]{1,0:T(8,128)S(1)}, f32[2,128]{1,0:T(2,128)S(1)}) custom-call(f32[12,256,256]{2,1,0:T(8,128)} %bitcast.4, s32[1,12]{1,0:T(1,128)} %bitcast.6, s32[1,12]{1,0:T(1,128)} %bitcast.7, s32[1,1]{1,0:T(1,128)S(6)} %copy.11.count_hbm, ...), custom_call_target="tpu_custom_call" | custom-call | tf_op jit(solution)/shard_map/pallas_call | solution.py:521
  21.2 1.2 %shard_map.104 = (f32[16,2048]{1,0:T(8,128)}, f32[16,16]{1,0:T(8,128)}, f32[16,16]{1,0:T(8,128)}) custom-call(f32[2,128]{1,0:T(2,128)S(1)} %get-tuple-element.8.sums_ref, f32[16,16]{1,0:T(8,128)S(1)} %get-tuple-element.9.alpha_t_ref, f32[16,16]{1,0:T(8,128)S(1)} %get-tuple-element.10.known_ref, f32[16,192]{1,0:T(8,128)S(1)} %get-tuple-element.11.wide_ref, ...), custom_call_target="tpu_custom_call" | custom-call | tf_op jit(solution)/shard_map/pallas_call | solution.py:573
